TPU v7x, 32 devices: a whole 2x2x4 slice. The times are simulated.
32 devices in a mesh: dp: 8 (over z, x), tensor: 4 (over y, core).
Axes of the slice: x: 2, y: 2, z: 4, core: 2. Of those that a mesh axis runs over, the one named last changes fastest.
Arguments:
- tokens: bfloat16 [8192, 2048], P(('dp', 'tensor')), may hold values from -6 to 6
- cotangent: bfloat16 [8192, 2048], P(('dp', 'tensor')), may hold values from -6 to 6
- norm1_gain: float32 [2048], replicated, may hold values from 0.5 to 1.5
- norm1_shift: float32 [2048], replicated, may hold values from -3 to 3
- query_weight: bfloat16 [2048, 2048], P('dp', 'tensor'), may hold values from -2 to 2
- query_bias: float32 [2048], replicated, may hold values from -5 to 5
- keyval_weight: bfloat16 [2048, 256], P('dp'), may hold values from -0.125 to 0.125
- value_bias: float32 [128], replicated, may hold values from -3 to 3
- out_weight: bfloat16 [2048, 2048], P('tensor', 'dp'), may hold values from -1.5 to 1.5
- out_bias: float32 [2048], replicated, may hold values from -3 to 3
- norm2_gain: float32 [2048], replicated, may hold values from 0.5 to 1.5
- norm2_shift: float32 [2048], replicated, may hold values from -3 to 3
- fc_weight: bfloat16 [2048, 8192], P('dp', 'tensor'), may hold values from -0.125 to 0.125
- fc_bias: float32 [8192], replicated, may hold values from -3 to 3
- proj_weight: bfloat16 [8192, 2048], P('tensor', 'dp'), may hold values from -0.0625 to 0.0625
- proj_bias: float32 [2048], replicated, may hold values from -3 to 3
Outputs:
- mixed: bfloat16 [8192, 2048], P(('dp', 'tensor'))
- token_grad: bfloat16 [8192, 2048], P(('dp', 'tensor'))
- norm1_gain_grad: float32 [2048], replicated
- norm1_shift_grad: float32 [2048], replicated
- query_weight_grad: float32 [2048, 2048], P('dp', 'tensor')
- query_bias_grad: float32 [2048], replicated
- keyval_weight_grad: float32 [2048, 256], P('dp')
- value_bias_grad: float32 [128], replicated
- out_weight_grad: float32 [2048, 2048], P('tensor', 'dp')
- out_bias_grad: float32 [2048], replicated
- norm2_gain_grad: float32 [2048], replicated
- norm2_shift_grad: float32 [2048], replicated
- fc_weight_grad: float32 [2048, 8192], P('dp', 'tensor')
- fc_bias_grad: float32 [8192], replicated
- proj_weight_grad: float32 [8192, 2048], P('tensor', 'dp')
- proj_bias_grad: float32 [2048], replicated
- clipped_query: bfloat16 [2048, 2048], P('dp', 'tensor')
- clipped_key: bfloat16 [2048, 128], P('dp')
All inputs are finite; a program needn't handle non-finite values.
Results may differ from a plain program's by a relative error of at most 0.02.
Values may be sent and summed in bfloat16 or wider, within the bound.
No kernel may reach another device: no remote copies, remote signals or barrier semaphores. Data moves between devices by JAX's collectives and lax.ppermute only.
A program may use at most 192 MiB of HBM per device.

v0:
```python
import jax
import jax.numpy as jnp
from jax import lax
from jax.sharding import PartitionSpec as P

HEADS = 16
HEAD_DIM = 128
SEQ_LEN = 1024
BLOCK = 256


CLIP_LIMIT = 3.0


def layer_norm(values, norm_gain, norm_shift):
    center = values - jnp.mean(values, axis=-1, keepdims=True)
    spread = jnp.mean(center * center, axis=-1, keepdims=True)
    return center * lax.rsqrt(spread + 1e-05) * norm_gain + norm_shift


def gelu_tanh(values):
    return (
        0.5
        * values
        * (1.0 + jnp.tanh(0.7978845608028654 * (values + 0.044715 * values * values * values)))
    )


def fetch_weights(query_weight, keyval_weight, out_weight, fc_weight, proj_weight):
    attention_parts = (
        lax.all_gather(query_weight, "dp", axis=0, tiled=True),
        lax.all_gather(keyval_weight, "dp", axis=0, tiled=True),
        lax.all_gather(out_weight, "dp", axis=1, tiled=True),
    )
    feed_parts = (
        lax.all_gather(fc_weight, "dp", axis=0, tiled=True),
        lax.all_gather(proj_weight, "dp", axis=1, tiled=True),
    )
    return (
        attention_parts[0],
        attention_parts[1],
        attention_parts[2],
        feed_parts[0],
        feed_parts[1],
    )


def block_scores(query_block, key_rows, start, total):
    scores = jnp.einsum(
        "qhd,kd->hqk", query_block, key_rows, preferred_element_type=jnp.float32
    ) * HEAD_DIM ** (-0.5)
    query_pos = start + jnp.arange(query_block.shape[0])
    key_pos = jnp.arange(total)
    same_sequence = (query_pos // SEQ_LEN)[:, None] == (key_pos // SEQ_LEN)[None, :]
    earlier = (key_pos % SEQ_LEN // BLOCK)[None, :] <= (query_pos % SEQ_LEN // BLOCK)[:, None]
    return jnp.where((same_sequence & earlier)[None], scores, -1e30)


def attend_forward(queries, keyval, heads):
    total = queries.shape[0]
    rows_block = min(512, total)
    key_rows = keyval[:, :HEAD_DIM]
    value_rows = keyval[:, HEAD_DIM:]

    def one_block(start):
        query_block = lax.dynamic_slice_in_dim(queries, start, rows_block, 0).reshape(
            rows_block, heads, HEAD_DIM
        )
        masked = block_scores(query_block, key_rows, start, total)
        highest = jnp.max(masked, axis=-1, keepdims=True)
        shifted = jnp.exp(masked - highest)
        totals = jnp.sum(shifted, axis=-1, keepdims=True)
        weights_low = (shifted / totals).astype(jnp.bfloat16)
        attended = jnp.einsum(
            "hqk,kd->qhd", weights_low, value_rows, preferred_element_type=jnp.float32
        )
        logsum = highest[..., 0] + jnp.log(totals[..., 0])
        return (
            attended.reshape(rows_block, heads * HEAD_DIM).astype(jnp.bfloat16),
            logsum,
            jnp.max(highest[..., 0], axis=1),
        )

    starts = jnp.arange(total // rows_block, dtype=jnp.int32) * rows_block
    attended, logsums, peaks = lax.map(one_block, starts)
    return (attended.reshape(total, heads * HEAD_DIM), logsums, jnp.max(peaks, axis=0))


def attend_backward(queries, keyval, logsums, attended_grad, heads):
    total = queries.shape[0]
    rows_block = min(512, total)
    key_rows = keyval[:, :HEAD_DIM]
    value_rows = keyval[:, HEAD_DIM:]
    scale = HEAD_DIM ** (-0.5)

    def one_block(carry, operands):
        start, logsum = operands
        query_block = lax.dynamic_slice_in_dim(queries, start, rows_block, 0).reshape(
            rows_block, heads, HEAD_DIM
        )
        grad_block = lax.dynamic_slice_in_dim(attended_grad, start, rows_block, 0).reshape(
            rows_block, heads, HEAD_DIM
        )
        masked = block_scores(query_block, key_rows, start, total)
        weights_soft = jnp.exp(masked - logsum[..., None])
        weights_low = weights_soft.astype(jnp.bfloat16)
        weight_grad = jnp.einsum(
            "qhd,kd->hqk", grad_block, value_rows, preferred_element_type=jnp.float32
        )
        inner = jnp.sum(weights_soft * weight_grad, axis=-1, keepdims=True)
        score_grad = (weights_soft * (weight_grad - inner)).astype(jnp.bfloat16)
        query_grad = (
            jnp.einsum("hqk,kd->qhd", score_grad, key_rows, preferred_element_type=jnp.float32)
            * scale
        )
        key_grad = (
            carry[0]
            + jnp.einsum("hqk,qhd->kd", score_grad, query_block, preferred_element_type=jnp.float32)
            * scale
        )
        value_grad = carry[1] + jnp.einsum(
            "hqk,qhd->kd", weights_low, grad_block, preferred_element_type=jnp.float32
        )
        return (
            (key_grad, value_grad),
            query_grad.reshape(rows_block, heads * HEAD_DIM).astype(jnp.bfloat16),
        )

    starts = jnp.arange(total // rows_block, dtype=jnp.int32) * rows_block
    empty = jnp.zeros((total, HEAD_DIM), jnp.float32)
    (key_grad, value_grad), query_grad = lax.scan(one_block, (empty, empty), (starts, logsums))
    return (key_grad, value_grad, query_grad.reshape(total, heads * HEAD_DIM))


def contract_rows(first_operand, second_operand):
    return jnp.einsum(
        "ti,td->id", first_operand, second_operand, preferred_element_type=jnp.float32
    )


def contract_cols(first_operand, second_operand):
    return jnp.einsum(
        "ti,di->td", first_operand, second_operand, preferred_element_type=jnp.float32
    )


def per_device(
    tokens,
    cotangent,
    norm1_gain,
    norm1_shift,
    query_weight,
    query_bias,
    keyval_weight,
    value_bias,
    out_weight,
    out_bias,
    norm2_gain,
    norm2_shift,
    fc_weight,
    fc_bias,
    proj_weight,
    proj_bias,
):
    width = tokens.shape[1]
    split = lax.axis_size("tensor")
    position = lax.axis_index("tensor")
    local_heads = HEADS // split
    query_cols = width // split
    hidden_cols = fc_bias.shape[0] // split
    own_rows = tokens.shape[0]
    local_qbias = lax.dynamic_slice_in_dim(query_bias, position * query_cols, query_cols)
    local_fbias = lax.dynamic_slice_in_dim(fc_bias, position * hidden_cols, hidden_cols)
    whole_query, whole_keyval, whole_out, whole_fc, whole_proj = fetch_weights(
        query_weight, keyval_weight, out_weight, fc_weight, proj_weight
    )
    residual = tokens.astype(jnp.float32)
    normed1 = lax.all_gather(
        layer_norm(residual, norm1_gain, norm1_shift).astype(jnp.bfloat16),
        "tensor",
        axis=0,
        tiled=True,
    )
    queries = (
        jnp.dot(normed1, whole_query, preferred_element_type=jnp.float32) + local_qbias
    ).astype(jnp.bfloat16)
    kv_shift = jnp.concatenate([jnp.zeros((HEAD_DIM,), jnp.float32), value_bias])
    keyval = (jnp.dot(normed1, whole_keyval, preferred_element_type=jnp.float32) + kv_shift).astype(
        jnp.bfloat16
    )
    attended, logsums, head_peaks = attend_forward(queries, keyval, local_heads)
    attn_terms = jnp.dot(attended, whole_out, preferred_element_type=jnp.float32)
    middle = (
        residual
        + lax.psum_scatter(
            attn_terms.astype(jnp.bfloat16), "tensor", scatter_dimension=0, tiled=True
        ).astype(jnp.float32)
        + out_bias
    )
    normed2 = lax.all_gather(
        layer_norm(middle, norm2_gain, norm2_shift).astype(jnp.bfloat16),
        "tensor",
        axis=0,
        tiled=True,
    )
    hidden = jnp.dot(normed2, whole_fc, preferred_element_type=jnp.float32) + local_fbias
    activated = gelu_tanh(hidden).astype(jnp.bfloat16)
    feed_terms = jnp.dot(activated, whole_proj, preferred_element_type=jnp.float32)
    mixed = (
        middle
        + lax.psum_scatter(
            feed_terms.astype(jnp.bfloat16), "tensor", scatter_dimension=0, tiled=True
        ).astype(jnp.float32)
        + proj_bias
    ).astype(jnp.bfloat16)
    peak_table = lax.dynamic_update_slice_in_dim(
        jnp.full((HEADS,), -1e30, jnp.float32), head_peaks, position * local_heads, 0
    )
    peak_table = lax.pmax(peak_table, ("dp", "tensor"))
    whole_query, whole_keyval, whole_out, whole_fc, whole_proj = fetch_weights(
        query_weight, keyval_weight, out_weight, fc_weight, proj_weight
    )
    out_grad = lax.all_gather(cotangent, "tensor", axis=0, tiled=True)
    proj_grad = contract_rows(activated, out_grad)
    activated_grad = contract_cols(out_grad, whole_proj)
    gelu_pull = jax.vjp(gelu_tanh, hidden)[1]
    hidden_grad = gelu_pull(activated_grad)[0].astype(jnp.bfloat16)
    fc_grad = contract_rows(normed2, hidden_grad)
    normed2_grad = lax.psum_scatter(
        contract_cols(hidden_grad, whole_fc).astype(jnp.bfloat16),
        "tensor",
        scatter_dimension=0,
        tiled=True,
    ).astype(jnp.float32)
    norm2_pull = jax.vjp(layer_norm, middle, norm2_gain, norm2_shift)[1]
    middle_part, gain2_grad, shift2_grad = norm2_pull(normed2_grad)
    middle_grad = cotangent.astype(jnp.float32) + middle_part
    branch_grad = middle_grad.astype(jnp.bfloat16)
    branch_rows = lax.all_gather(branch_grad, "tensor", axis=0, tiled=True)
    out_grad_weight = contract_rows(attended, branch_rows)
    attended_grad = contract_cols(branch_rows, whole_out).astype(jnp.bfloat16)
    key_grad, value_grad, query_grad = attend_backward(
        queries, keyval, logsums, attended_grad, local_heads
    )
    key_grad, value_grad = (
        lax.psum(key_grad.astype(jnp.bfloat16), "tensor").astype(jnp.float32),
        lax.psum(value_grad.astype(jnp.bfloat16), "tensor").astype(jnp.float32),
    )
    keyval_grad = jnp.concatenate([key_grad, value_grad], axis=1).astype(jnp.bfloat16)
    query_grad_weight = contract_rows(normed1, query_grad)
    keyval_grad_weight = contract_rows(normed1, keyval_grad)
    keyval_own = lax.dynamic_slice_in_dim(keyval_grad, position * own_rows, own_rows, 0)
    normed1_grad = lax.psum_scatter(
        contract_cols(query_grad, whole_query).astype(jnp.bfloat16),
        "tensor",
        scatter_dimension=0,
        tiled=True,
    ).astype(jnp.float32)
    normed1_grad = normed1_grad + contract_cols(keyval_own, whole_keyval)
    norm1_pull = jax.vjp(layer_norm, residual, norm1_gain, norm1_shift)[1]
    residual_part, gain1_grad, shift1_grad = norm1_pull(normed1_grad)
    token_grad = (middle_grad + residual_part).astype(jnp.bfloat16)
    weight_sums = (
        lax.psum_scatter(
            query_grad_weight.astype(jnp.bfloat16), "dp", scatter_dimension=0, tiled=True
        ).astype(jnp.float32),
        lax.psum_scatter(
            keyval_grad_weight.astype(jnp.bfloat16), "dp", scatter_dimension=0, tiled=True
        ).astype(jnp.float32),
        lax.psum_scatter(
            out_grad_weight.astype(jnp.bfloat16), "dp", scatter_dimension=1, tiled=True
        ).astype(jnp.float32),
        lax.psum_scatter(
            fc_grad.astype(jnp.bfloat16), "dp", scatter_dimension=0, tiled=True
        ).astype(jnp.float32),
        lax.psum_scatter(
            proj_grad.astype(jnp.bfloat16), "dp", scatter_dimension=1, tiled=True
        ).astype(jnp.float32),
    )
    query_bias_part = lax.dynamic_update_slice_in_dim(
        jnp.zeros((width,), jnp.float32),
        jnp.sum(query_grad, axis=0, dtype=jnp.float32),
        position * query_cols,
        0,
    )
    fc_bias_part = lax.dynamic_update_slice_in_dim(
        jnp.zeros((fc_bias.shape[0],), jnp.float32),
        jnp.sum(hidden_grad, axis=0, dtype=jnp.float32),
        position * hidden_cols,
        0,
    )
    value_bias_part = jnp.sum(keyval_own[:, HEAD_DIM:], axis=0, dtype=jnp.float32)
    out_bias_part = jnp.sum(branch_grad, axis=0, dtype=jnp.float32)
    proj_bias_part = jnp.sum(cotangent, axis=0, dtype=jnp.float32)
    small_sums = lax.psum(
        (
            gain1_grad,
            shift1_grad,
            gain2_grad,
            shift2_grad,
            out_bias_part,
            proj_bias_part,
            query_bias_part,
            value_bias_part,
            fc_bias_part,
        ),
        ("dp", "tensor"),
    )
    clip_factor = CLIP_LIMIT / jnp.maximum(peak_table, CLIP_LIMIT)
    key_factor = jnp.sqrt(jnp.min(clip_factor))
    local_clip = lax.dynamic_slice_in_dim(clip_factor, position * local_heads, local_heads)
    column_factor = jnp.repeat(local_clip / key_factor, HEAD_DIM)
    clipped_query = (query_weight.astype(jnp.float32) * column_factor[None, :]).astype(jnp.bfloat16)
    clipped_key = (keyval_weight[:, :HEAD_DIM].astype(jnp.float32) * key_factor).astype(
        jnp.bfloat16
    )
    return (
        mixed,
        token_grad,
        small_sums[0],
        small_sums[1],
        weight_sums[0],
        small_sums[6],
        weight_sums[1],
        small_sums[7],
        weight_sums[2],
        small_sums[4],
        small_sums[2],
        small_sums[3],
        weight_sums[3],
        small_sums[8],
        weight_sums[4],
        small_sums[5],
        clipped_query,
        clipped_key,
    )


def solution(mesh):
    return jax.shard_map(
        per_device,
        mesh=mesh,
        in_specs=(
            P(("dp", "tensor"), None),
            P(("dp", "tensor"), None),
            P(),
            P(),
            P("dp", "tensor"),
            P(),
            P("dp", None),
            P(),
            P("tensor", "dp"),
            P(),
            P(),
            P(),
            P("dp", "tensor"),
            P(),
            P("tensor", "dp"),
            P(),
        ),
        out_specs=(
            P(("dp", "tensor"), None),
            P(("dp", "tensor"), None),
            P(),
            P(),
            P("dp", "tensor"),
            P(),
            P("dp", None),
            P(),
            P("tensor", "dp"),
            P(),
            P(),
            P(),
            P("dp", "tensor"),
            P(),
            P("tensor", "dp"),
            P(),
            P("dp", "tensor"),
            P("dp", None),
        ),
        check_vma=False,
    )
```

profile of v0, /device:TPU:8, one launch (start us, length us, event | category | flops | bytes accessed | tf_op | source)
XLA Modules:
  0.0 1527.5 jit_solution(9412593056787642240)
XLA Ops:
  12.2 2.7 fusion.83
  17.1 33.3 %all-gather.14.cloned.1.call-done = bf16[2048,256]{1,0:T(8,128)(2,1)} async-done(((bf16[256,256]{1,0:T(8,128)(2,1)}), bf16[2048,256]{1,0:T(8,128)(2,1)}) %all-gather.14.cloned.1.call-update) | async-done | bytes 1048592 | tf_op jit(solution)/shard_map/all_gather | solution.py:32
  50.4 36.5 %all-gather.10.cloned.1.call-done = bf16[1024,2048]{1,0:T(8,128)(2,1)} async-done(((bf16[256,2048]{1,0:T(8,128)(2,1)}), bf16[1024,2048]{1,0:T(8,128)(2,1)}) %all-gather.10.cloned.1.call-update) | async-done | bytes 4194320 | tf_op jit(solution)/shard_map/all_gather | solution.py:178
  86.9 3.7 fusion.93
  90.9 47.3 %all-gather.12.cloned.1.call-done = bf16[2048,512]{1,0:T(8,128)(2,1)} async-done(((bf16[256,512]{1,0:T(8,128)(2,1)}), bf16[2048,512]{1,0:T(8,128)(2,1)}) %all-gather.12.cloned.1.call-update) | async-done | bytes 2097168 | tf_op jit(solution)/shard_map/all_gather | solution.py:31
  138.2 5.2 add_convert_fusion.3
  144.0 38.9 %while.35 = (s32[]{:T(128)}, bf16[2,512,512]{2,1,0:T(8,128)(2,1)}, f32[2,4,512]{2,1,0:T(4,128)S(1)}, f32[2,4]{1,0:T(2,128)S(1)}, s32[2]{0:T(128)S(1)}, /*index=5...) while((s32[]{:T(128)}, bf16[2,512,512]{2,1,0:T(8,128)(2,1)}, ...), condition=%wide.region_6.7_spmd, body=%wide.region_2.6_spmd.sunk | while | flops 1107077632 | bytes 108093728 | solution.py:85
  148.0 1.9 bitcast_reduce_fusion.2
  149.9 1.9 fusion.164
  153.2 4.8 fusion.162
  159.0 3.3 fusion.163
  167.4 1.9 bitcast_reduce_fusion.2
  169.3 1.9 fusion.164
  172.6 4.9 fusion.162
  178.5 3.3 fusion.163
  182.9 4.3 all-gather.16.cloned.1.call-done
  187.2 6.2 convolution_convert_fusion.5
  194.6 43.6 %reduce-scatter.10.cloned.1.call-done = bf16[256,2048]{1,0:T(8,128)(2,1)} async-done(((bf16[1024,2048]{1,0:T(8,128)(2,1)}), bf16[256,2048]{1,0:T(8,128)(2,1)}) %reduce-scatter.10.cloned.1.call-update) | async-done | bytes 1048592 | tf_op jit(solution)/shard_map/reduce_scatter | solution.py:195
  239.9 1.8 multiply_reduce_fusion
  245.7 117.2 %all-gather.20.cloned.1.call-done = bf16[2048,2048]{1,0:T(8,128)(2,1)} async-done(((bf16[256,2048]{1,0:T(8,128)(2,1)}), bf16[2048,2048]{1,0:T(8,128)(2,1)}) %all-gather.20.cloned.1.call-update) | async-done | bytes 8388624 | tf_op jit(solution)/shard_map/all_gather | solution.py:36
  362.8 36.7 %all-gather.18.cloned.1.call-done = bf16[1024,2048]{1,0:T(8,128)(2,1)} async-done(((bf16[256,2048]{1,0:T(8,128)(2,1)}), bf16[1024,2048]{1,0:T(8,128)(2,1)}) %all-gather.18.cloned.1.call-update) | async-done | bytes 4194320 | tf_op jit(solution)/shard_map/all_gather | solution.py:200
  399.5 14.4 fusion.105
  413.9 21.7 %all-gather.24.cloned.1.call-done = bf16[1024,2048]{1,0:T(8,128)(2,1)} async-done(((bf16[256,2048]{1,0:T(8,128)(2,1)}), bf16[1024,2048]{1,0:T(8,128)(2,1)}) %all-gather.24.cloned.1.call-update) | async-done | bytes 4194320 | tf_op jit(solution)/shard_map/all_gather | solution.py:223
  435.6 125.2 %all-gather.22.cloned.1.call-done = bf16[2048,2048]{1,0:T(8,128)(2,1)} async-done(((bf16[2048,256]{1,0:T(8,128)(2,1)}), bf16[2048,2048]{1,0:T(8,128)(2,1)}) %all-gather.22.cloned.1.call-update) | async-done | bytes 8388624 | tf_op jit(solution)/shard_map/all_gather | solution.py:37
  560.7 20.5 %convert_reduce_fusion = (f32[2048]{0:T(1024)}, bf16[1024,2048]{1,0:T(8,128)(2,1)S(1)}) fusion(f32[1024,2048]{1,0:T(8,128)} %fusion.105, f32[2048]{0:T(1024)S(1)} %dynamic_slice.57, bf16[1024,2048]{1,0:T(8,128)(2,1)} %all-gather.24.cloned.1.call-done, bf16[2048,2048]{1,0:T(8,128)(2,1)} %all-gather.22.cloned.1.call-done), kind=kOutput, calls=%fused_computation.131 | convolution fusion | flops 8646555648 | bytes 25182208 | tf_op jit(solution)/shard_map/ti,di->td/dot_general | solution.py:142
  581.2 2.1 copy-done.40
  583.2 13.0 convolution_convert_fusion.3
  596.3 15.9 %convolution_convert_fusion.4 = bf16[1024,2048]{1,0:T(8,128)(2,1)} fusion(bf16[2048,2048]{1,0:T(8,128)(2,1)} %all-gather.22.cloned.1.call-done, f32[1024,2048]{1,0:T(8,128)} %fusion.105, f32[2048]{0:T(1024)S(1)} %dynamic_slice.57), kind=kOutput, calls=%fused_computation.137 | convolution fusion | flops 8613003264 | bytes 20979712 | tf_op jit(solution)/shard_map/dot_general | solution.py:208
  612.3 28.7 %reduce-scatter.14.cloned.1.call-done = bf16[256,2048]{1,0:T(8,128)(2,1)} async-done(((bf16[1024,2048]{1,0:T(8,128)(2,1)}), bf16[256,2048]{1,0:T(8,128)(2,1)}) %reduce-scatter.14.cloned.1.call-update) | async-done | bytes 1048592 | tf_op jit(solution)/shard_map/reduce_scatter | solution.py:229
  641.0 2.9 fusion.89
  643.9 44.2 %reduce-scatter.12.cloned.1.call-done = bf16[256,2048]{1,0:T(8,128)(2,1)} async-done(((bf16[1024,2048]{1,0:T(8,128)(2,1)}), bf16[256,2048]{1,0:T(8,128)(2,1)}) %reduce-scatter.12.cloned.1.call-update) | async-done | bytes 1048592 | tf_op jit(solution)/shard_map/reduce_scatter | solution.py:211
  688.1 3.7 fusion.103
  693.2 2.0 convert_reduce_fusion.4
  696.1 33.7 %all-gather.26.cloned.1.call-done = bf16[1024,2048]{1,0:T(8,128)(2,1)} async-done(((bf16[256,2048]{1,0:T(8,128)(2,1)}), bf16[1024,2048]{1,0:T(8,128)(2,1)}) %all-gather.26.cloned.1.call-update) | async-done | bytes 4194320 | tf_op jit(solution)/shard_map/all_gather | solution.py:239
  729.8 6.2 convolution_convert_fusion.9
  736.0 41.8 %while.36 = (s32[]{:T(128)}, f32[1024,128]{1,0:T(8,128)S(1)}, f32[1024,128]{1,0:T(8,128)}, bf16[2,512,512]{1,2,0:T(8,128)(2,1)}, s32[2]{0:T(128)S(1)}, /*index=5...) while((s32[]{:T(128)}, f32[1024,128]{1,0:T(8,128)S(1)}, ...), condition=%wide.region_16.17_spmd.clone, body=%wide.region_14.16_spmd.clone.sunk | while | flops 2718607872 | bytes 88424808 | solution.py:131
  741.6 2.3 fusion.174
  743.9 2.9 fusion.178
  746.8 3.7 fusion.175
  750.5 2.4 fusion.176
  762.4 2.3 fusion.174
  764.7 2.9 fusion.178
  767.6 3.7 fusion.175
  771.3 2.4 fusion.176
  780.0 1.8 convert_element_type.206
  781.8 5.9 convolution_convert_fusion.2
  787.8 16.4 %convolution_convert_fusion = bf16[2048,2048]{1,0:T(8,128)(2,1)} fusion(bf16[1024,2048]{1,0:T(8,128)(2,1)} %all-gather.24.cloned.1.call-done, f32[1024,2048]{1,0:T(8,128)} %fusion.105, f32[2048]{0:T(1024)S(1)} %dynamic_slice.57), kind=kOutput, calls=%fused_computation.133 | convolution fusion | flops 8615100416 | bytes 20979712 | tf_op jit(solution)/shard_map/ti,td->id/dot_general | solution.py:136
  804.3 14.1 convolution_convert_fusion.1
  821.3 4.6 convolution_convert_fusion.8
  826.2 6.6 convolution_convert_fusion.6
  833.0 6.1 convolution_convert_fusion.7
  839.4 40.4 %pmax.7 = f32[16]{0:T(128)S(1)} all-reduce(f32[16]{0:T(128)S(1)} %dynamic_update_slice.42), channel_id=1, replica_groups=mesh['dp'=8,'tensor'=4] {'dp','tensor'}, use_global_device_ids=true, to_apply=%region_46.47 | all-reduce | flops 16 | bytes 128 | tf_op jit(solution)/shard_map/pmax | solution.py:219
  884.3 3.2 fusion.99
  889.0 2.7 convert_reduce_fusion.3
  892.4 121.2 %reduce-scatter.26.cloned.1.call-done = bf16[2048,256]{1,0:T(8,128)(2,1)} async-done(((bf16[2048,2048]{1,0:T(8,128)(2,1)}), bf16[2048,256]{1,0:T(8,128)(2,1)}) %reduce-scatter.26.cloned.1.call-update) | async-done | bytes 1048592 | tf_op jit(solution)/shard_map/reduce_scatter | solution.py:276
  1013.5 2.7 convert_element_type.221
  1016.2 147.4 %reduce-scatter.24.cloned.1.call-done = bf16[256,2048]{1,0:T(8,128)(2,1)} async-done(((bf16[2048,2048]{1,0:T(8,128)(2,1)}), bf16[256,2048]{1,0:T(8,128)(2,1)}) %reduce-scatter.24.cloned.1.call-update) | async-done | bytes 1048592 | tf_op jit(solution)/shard_map/reduce_scatter | solution.py:273
  1163.7 2.8 convert_element_type.218
  1166.4 64.6 %reduce-scatter.20.cloned.1.call-done = bf16[256,256]{1,0:T(8,128)(2,1)} async-done(((bf16[2048,256]{1,0:T(8,128)(2,1)}), bf16[256,256]{1,0:T(8,128)(2,1)}) %reduce-scatter.20.cloned.1.call-update) | async-done | bytes 131088 | tf_op jit(solution)/shard_map/reduce_scatter | solution.py:267
  1232.7 69.3 %reduce-scatter.22.cloned.1.call-done = bf16[512,256]{1,0:T(8,128)(2,1)} async-done(((bf16[512,2048]{1,0:T(8,128)(2,1)}), bf16[512,256]{1,0:T(8,128)(2,1)}) %reduce-scatter.22.cloned.1.call-update) | async-done | bytes 262160 | tf_op jit(solution)/shard_map/reduce_scatter | solution.py:270
  1302.0 1.8 convert_element_type.215
  1303.7 69.2 %reduce-scatter.18.cloned.1.call-done = bf16[256,512]{1,0:T(8,128)(2,1)} async-done(((bf16[2048,512]{1,0:T(8,128)(2,1)}), bf16[256,512]{1,0:T(8,128)(2,1)}) %reduce-scatter.18.cloned.1.call-update) | async-done | bytes 262160 | tf_op jit(solution)/shard_map/reduce_scatter | solution.py:264
  1372.9 1.8 convert_element_type.209
  1374.7 134.3 %all-reduce.6.cloned.1.call-done = (f32[2048]{0:T(1024)}, f32[2048]{0:T(1024)}, f32[2048]{0:T(1024)}, f32[128]{0:T(128)}, f32[2048]{0:T(1024)}, /*index=5*/f32[2...) async-done(((f32[2048]{0:T(1024)}, f32[2048]{0:T(1024)}, f32[2048]{0:T(1024)}, f32[128]{0:T(128)}, f32[2048]{0:T(1024)}, /*index=5*/f32[2048]{0:T(1024)}, ...) | async-done | bytes 90640 | tf_op jit(solution)/shard_map/psum | solution.py:295
  (232 shorter events, 67.8 us)
Async XLA Ops:
  7.2 9.1 copy-start.38
  7.2 43.2 %all-gather.14.cloned.1.call-start = ((), (), s32[]{:S(2)}) async-start(), calls=%async_computation.11 | async-start | bytes 1179648 | tf_op jit(solution)/shard_map/all_gather | solution.py:32
  7.9 79.0 %all-gather.10.cloned.1.call-start = ((), (), s32[]{:S(2)}) async-start(), calls=%async_computation.9 | async-start | bytes 5242880 | tf_op jit(solution)/shard_map/all_gather | solution.py:178
  9.4 2.2 copy-start.24
  14.9 123.3 %all-gather.12.cloned.1.call-start = ((), (), s32[]{:S(2)}) async-start(), calls=%async_computation.10 | async-start | bytes 2359296 | tf_op jit(solution)/shard_map/all_gather | solution.py:31
  15.7 171.5 %all-gather.16.cloned.1.call-start = ((), (), s32[]{:S(2)}) async-start(), calls=%async_computation.12 | async-start | bytes 2359296 | tf_op jit(solution)/shard_map/all_gather | solution.py:33
  16.2 222.0 %reduce-scatter.10.cloned.1.call-start = ((), (), s32[]{:S(2)}) async-start(), calls=%async_computation.13 | async-start | bytes 5242880 | tf_op jit(solution)/shard_map/reduce_scatter | solution.py:195
  90.7 47.5 %copy-start.7 = (bf16[1024,128]{1,0:T(8,128)(2,1)}, bf16[1024,128]{1,0:T(8,128)(2,1)S(1)}, u32[]{:S(2)}) copy-start(bf16[1024,128]{1,0:T(8,128)(2,1)S(1)} %get-tuple-element.655) | copy-start | bytes 786436
  149.9 3.2 copy-start
  153.2 5.8 copy-start.1
  169.3 3.2 copy-start
  172.6 5.9 copy-start.1
  182.9 10.6 copy-start.36
  193.4 44.8 %copy-start.2 = (bf16[256,2048]{1,0:T(8,128)(2,1)S(1)}, bf16[256,2048]{1,0:T(8,128)(2,1)}, u32[]{:S(2)}) copy-start(bf16[256,2048]{1,0:T(8,128)(2,1)} %param.20) | copy-start | bytes 3145732
  193.4 44.8 %copy-start.20 = (f32[2048]{0:T(1024)S(1)}, f32[2048]{0:T(1024)}, u32[]{:S(2)}) copy-start(f32[2048]{0:T(1024)} %param.29) | copy-start | bytes 24580
  193.4 48.3 %copy-start.23 = (f32[2048]{0:T(1024)S(1)}, f32[2048]{0:T(1024)}, u32[]{:S(2)}) copy-start(f32[2048]{0:T(1024)} %param.30) | copy-start | bytes 24580
  193.4 48.3 %copy-start.33 = (f32[2048]{0:T(1024)S(1)}, f32[2048]{0:T(1024)}, u32[]{:S(2)}) copy-start(f32[2048]{0:T(1024)} %param.31) | copy-start | bytes 24580
  193.5 169.4 %all-gather.20.cloned.1.call-start = ((), (), s32[]{:S(2)}) async-start(), calls=%async_computation.15 | async-start | bytes 9437184 | tf_op jit(solution)/shard_map/all_gather | solution.py:36
  194.0 205.5 %all-gather.18.cloned.1.call-start = ((), (), s32[]{:S(2)}) async-start(), calls=%async_computation.14 | async-start | bytes 5242880 | tf_op jit(solution)/shard_map/all_gather | solution.py:200
  238.2 3.6 copy-start.4
  243.4 192.1 %all-gather.24.cloned.1.call-start = ((), (), s32[]{:S(2)}) async-start(), calls=%async_computation.18 | async-start | bytes 5242880 | tf_op jit(solution)/shard_map/all_gather | solution.py:223
  244.2 316.5 %all-gather.22.cloned.1.call-start = ((), (), s32[]{:S(2)}) async-start(), calls=%async_computation.16 | async-start | bytes 9437184 | tf_op jit(solution)/shard_map/all_gather | solution.py:37
  244.9 396.1 %reduce-scatter.14.cloned.1.call-start = ((), (), s32[]{:S(2)}) async-start(), calls=%async_computation.19 | async-start | bytes 5242880 | tf_op jit(solution)/shard_map/reduce_scatter | solution.py:229
  581.2 2.1 copy-start.40
  596.2 91.9 %reduce-scatter.12.cloned.1.call-start = ((), (), s32[]{:S(2)}) async-start(), calls=%async_computation.17 | async-start | bytes 5242880 | tf_op jit(solution)/shard_map/reduce_scatter | solution.py:211
  612.2 75.9 %copy-start.35 = (f32[2048]{0:T(1024)S(1)}, f32[2048]{0:T(1024)}, u32[]{:S(2)}) copy-start(f32[2048]{0:T(1024)} %param.35) | copy-start | bytes 24580
  612.3 117.5 %all-gather.26.cloned.1.call-start = ((), (), s32[]{:S(2)}) async-start(), calls=%async_computation.20 | async-start | bytes 5242880 | tf_op jit(solution)/shard_map/all_gather | solution.py:239
  688.1 5.0 copy-start.10
  691.8 1.3 copy-start.5
  691.9 3.4 copy-start.29
  695.2 123.3 %all-reduce.8.cloned.1.call-start = ((), (), s32[]{:S(2)}) async-start(), calls=%async_computation.28 | async-start | bytes 1048576 | tf_op jit(solution)/shard_map/psum | solution.py:246
  696.1 39.9 %copy-start.8 = (bf16[1024,128]{1,0:T(8,128)(2,1)S(1)}, bf16[1024,128]{1,0:T(8,128)(2,1)}, u32[]{:S(2)}) copy-start(bf16[1024,128]{1,0:T(8,128)(2,1)} %copy-done.7) | copy-start | bytes 786436
  741.6 2.3 copy-start.16
  746.8 3.7 copy-start.17
  752.9 1.4 copy-start.9
  754.4 1.5 copy-start.12
  756.0 1.0 copy-start.13
  762.4 2.3 copy-start.16
  767.6 3.7 copy-start.17
  773.7 1.4 copy-start.9
  775.2 1.5 copy-start.12
  781.8 102.5 %reduce-scatter.16.cloned.1.call-start = ((), (), s32[]{:S(2)}) async-start(), calls=%async_computation.21 | async-start | bytes 5242880 | tf_op jit(solution)/shard_map/reduce_scatter | solution.py:253
  787.8 225.8 %reduce-scatter.26.cloned.1.call-start = ((), (), s32[]{:S(2)}) async-start(), calls=%async_computation.26 | async-start | bytes 9437184 | tf_op jit(solution)/shard_map/reduce_scatter | solution.py:276
  804.3 359.4 %reduce-scatter.24.cloned.1.call-start = ((), (), s32[]{:S(2)}) async-start(), calls=%async_computation.25 | async-start | bytes 9437184 | tf_op jit(solution)/shard_map/reduce_scatter | solution.py:273
  818.4 412.7 %reduce-scatter.20.cloned.1.call-start = ((), (), s32[]{:S(2)}) async-start(), calls=%async_computation.23 | async-start | bytes 1179648 | tf_op jit(solution)/shard_map/reduce_scatter | solution.py:267
  821.3 4.9 copy-start.39
  825.9 476.0 %reduce-scatter.22.cloned.1.call-start = ((), (), s32[]{:S(2)}) async-start(), calls=%async_computation.24 | async-start | bytes 2359296 | tf_op jit(solution)/shard_map/reduce_scatter | solution.py:270
  832.8 6.3 copy-start.37
  832.9 48.4 %copy-start.15 = (bf16[256,512]{1,0:T(8,128)(2,1)S(1)}, bf16[256,512]{1,0:T(8,128)(2,1)}, u32[]{:S(2)}) copy-start(bf16[256,512]{1,0:T(8,128)(2,1)} %param.24) | copy-start | bytes 786436
  832.9 49.2 %copy-start.34 = (f32[2048]{0:T(1024)S(1)}, f32[2048]{0:T(1024)}, u32[]{:S(2)}) copy-start(f32[2048]{0:T(1024)} %get-tuple-element.455) | copy-start | bytes 24580
  832.9 49.5 %copy-start.14 = (bf16[2,512,512]{1,2,0:T(8,128)(2,1)S(1)}, bf16[2,512,512]{1,2,0:T(8,128)(2,1)}, u32[]{:S(2)}) copy-start(bf16[2,512,512]{1,2,0:T(8,128)(2,1)} %get-tuple-element.326) | copy-start | bytes 3145732
  832.9 51.4 %copy-start.3 = (bf16[256,2048]{1,0:T(8,128)(2,1)S(1)}, bf16[256,2048]{1,0:T(8,128)(2,1)}, u32[]{:S(2)}) copy-start(bf16[256,2048]{1,0:T(8,128)(2,1)} %param.20) | copy-start | bytes 3145732
  832.9 51.4 %copy-start.22 = (f32[2048]{0:T(1024)S(1)}, f32[2048]{0:T(1024)}, u32[]{:S(2)}) copy-start(f32[2048]{0:T(1024)} %param.22) | copy-start | bytes 24580
  832.9 51.4 %copy-start.25 = (f32[256]{0:T(256)S(1)}, f32[256]{0:T(256)}, u32[]{:S(2)}) copy-start(f32[256]{0:T(256)} %copy-done.24) | copy-start | bytes 3076
  832.9 540.0 %reduce-scatter.18.cloned.1.call-start = ((), (), s32[]{:S(2)}) async-start(), calls=%async_computation.22 | async-start | bytes 2359296 | tf_op jit(solution)/shard_map/reduce_scatter | solution.py:264
  839.0 48.4 %copy-start.32 = (f32[256]{0:T(256)S(1)}, f32[256]{0:T(256)}, u32[]{:S(2)}) copy-start(f32[256]{0:T(256)} %copy-done.31) | copy-start | bytes 3076
  839.0 48.4 %copy-start.28 = (f32[256]{0:T(256)S(1)}, f32[256]{0:T(256)}, u32[]{:S(2)}) copy-start(f32[256]{0:T(256)} %copy-done.27) | copy-start | bytes 3076
  839.1 669.9 %all-reduce.6.cloned.1.call-start = ((), (), s32[]{:S(2)}) async-start(), calls=%async_computation.27 | async-start | bytes 181248 | tf_op jit(solution)/shard_map/psum | solution.py:295
  882.3 6.6 copy-start.21
  882.8 6.1 copy-start.26
  884.3 4.7 copy-start.6
  884.3 4.7 copy-start.30
  884.3 4.7 copy-start.11
  889.0 2.8 copy-start.19
  (4 other events, 2.9 us)
Sparse Core Ops, SparseCore 0:
  10.1 40.2 all-gather.13
  52.6 34.3 all-gather.9
  89.1 49.1 all-gather.11
  140.1 47.0 all-gather.15
  193.6 44.5 reduce-scatter.9
  240.2 122.6 all-gather.19
  365.0 34.4 all-gather.17
  401.1 34.4 all-gather.23
  437.6 123.0 all-gather.21
  596.4 44.5 reduce-scatter.13
  643.5 44.5 reduce-scatter.11
  695.3 34.4 all-gather.25
  781.9 33.4 all-reduce.7
  817.8 45.3 reduce-scatter.15
  866.7 146.7 reduce-scatter.25
  1017.0 146.5 reduce-scatter.23
  1166.9 64.1 reduce-scatter.19
  1234.4 67.4 reduce-scatter.21
  1305.5 67.3 reduce-scatter.17
  1380.3 128.5 all-reduce.5
where the time goes:
time: 1540 us; the launch traced here: 1530 us
  waiting for transfers between devices  1180 us (77%)
  matrix products  176 us (11%)
  other arithmetic  63.5 us (4%)
  blocking collectives  40.4 us (3%)
  local copies, waits for them, and re-layouts  39.8 us (3%)
  between operations  15.7 us (1%)
    reduce_scatter x1, waiting for transfers between devices, per_device(): lax.psum_scatter(fc_grad.astype(jnp.bfloat16), 'dp', scatter_dimension=0,...  147 us
    psum x1, waiting for transfers between devices, per_device(): lax.psum((gain1_grad, shift1_grad, gain2_grad, shift2_grad, out_bias_part...  134 us
    all_gather x1, waiting for transfers between devices, fetch_weights(): lax.all_gather(proj_weight, 'dp', axis=1, tiled=True)  125 us
    reduce_scatter x1, waiting for transfers between devices, per_device(): lax.psum_scatter(proj_grad.astype(jnp.bfloat16), 'dp', scatter_dimension=...  121 us
    all_gather x1, waiting for transfers between devices, fetch_weights(): lax.all_gather(fc_weight, 'dp', axis=0, tiled=True)  117 us
    reduce_scatter x1, waiting for transfers between devices, per_device(): lax.psum_scatter(out_grad_weight.astype(jnp.bfloat16), 'dp', scatter_dime...  69.3 us
    reduce_scatter x1, waiting for transfers between devices, per_device(): lax.psum_scatter(query_grad_weight.astype(jnp.bfloat16), 'dp', scatter_di...  69.2 us
    reduce_scatter x1, waiting for transfers between devices, per_device(): lax.psum_scatter(keyval_grad_weight.astype(jnp.bfloat16), 'dp', scatter_d...  64.6 us
  transfers between devices with their start and end apart: 20, of which 18 were waited for; matrix products, arithmetic and copies ran while one was open for 11% of the time, Pallas kernels for 0%

commit v1 on v0

v1 whole, which is shorter than its diff:
```python
import jax
import jax.numpy as jnp
from jax import lax
from jax.sharding import PartitionSpec as P


HEADS = 16
HEAD_DIM = 128
SEQ_LEN = 1024
BLOCK = 256


CLIP_LIMIT = 3.0


def layer_norm(values, norm_gain, norm_shift):
    center = values - jnp.mean(values, axis=-1, keepdims=True)
    spread = jnp.mean(center * center, axis=-1, keepdims=True)
    return center * lax.rsqrt(spread + 1e-05) * norm_gain + norm_shift


def gelu_tanh(values):
    return (
        0.5
        * values
        * (1.0 + jnp.tanh(0.7978845608028654 * (values + 0.044715 * values * values * values)))
    )


def block_scores(query_block, key_rows, start, total):
    scores = jnp.einsum(
        "qhd,kd->hqk", query_block, key_rows, preferred_element_type=jnp.float32
    ) * HEAD_DIM ** (-0.5)
    query_pos = start + jnp.arange(query_block.shape[0])
    key_pos = jnp.arange(total)
    same_sequence = (query_pos // SEQ_LEN)[:, None] == (key_pos // SEQ_LEN)[None, :]
    earlier = (key_pos % SEQ_LEN // BLOCK)[None, :] <= (query_pos % SEQ_LEN // BLOCK)[:, None]
    return jnp.where((same_sequence & earlier)[None], scores, -1e30)


def attend_forward(queries, keyval, heads):
    total = queries.shape[0]
    rows_block = min(512, total)
    key_rows = keyval[:, :HEAD_DIM]
    value_rows = keyval[:, HEAD_DIM:]

    def one_block(start):
        query_block = lax.dynamic_slice_in_dim(queries, start, rows_block, 0).reshape(
            rows_block, heads, HEAD_DIM
        )
        masked = block_scores(query_block, key_rows, start, total)
        highest = jnp.max(masked, axis=-1, keepdims=True)
        shifted = jnp.exp(masked - highest)
        totals = jnp.sum(shifted, axis=-1, keepdims=True)
        weights_low = (shifted / totals).astype(jnp.bfloat16)
        attended = jnp.einsum(
            "hqk,kd->qhd", weights_low, value_rows, preferred_element_type=jnp.float32
        )
        logsum = highest[..., 0] + jnp.log(totals[..., 0])
        return (
            attended.reshape(rows_block, heads * HEAD_DIM).astype(jnp.bfloat16),
            logsum,
            jnp.max(highest[..., 0], axis=1),
        )

    starts = jnp.arange(total // rows_block, dtype=jnp.int32) * rows_block
    attended, logsums, peaks = lax.map(one_block, starts)
    return (attended.reshape(total, heads * HEAD_DIM), logsums, jnp.max(peaks, axis=0))


def attend_backward(queries, keyval, logsums, attended_grad, heads):
    total = queries.shape[0]
    rows_block = min(512, total)
    key_rows = keyval[:, :HEAD_DIM]
    value_rows = keyval[:, HEAD_DIM:]
    scale = HEAD_DIM ** (-0.5)

    def one_block(carry, operands):
        start, logsum = operands
        query_block = lax.dynamic_slice_in_dim(queries, start, rows_block, 0).reshape(
            rows_block, heads, HEAD_DIM
        )
        grad_block = lax.dynamic_slice_in_dim(attended_grad, start, rows_block, 0).reshape(
            rows_block, heads, HEAD_DIM
        )
        masked = block_scores(query_block, key_rows, start, total)
        weights_soft = jnp.exp(masked - logsum[..., None])
        weights_low = weights_soft.astype(jnp.bfloat16)
        weight_grad = jnp.einsum(
            "qhd,kd->hqk", grad_block, value_rows, preferred_element_type=jnp.float32
        )
        inner = jnp.sum(weights_soft * weight_grad, axis=-1, keepdims=True)
        score_grad = (weights_soft * (weight_grad - inner)).astype(jnp.bfloat16)
        query_grad = (
            jnp.einsum("hqk,kd->qhd", score_grad, key_rows, preferred_element_type=jnp.float32)
            * scale
        )
        key_grad = (
            carry[0]
            + jnp.einsum("hqk,qhd->kd", score_grad, query_block, preferred_element_type=jnp.float32)
            * scale
        )
        value_grad = carry[1] + jnp.einsum(
            "hqk,qhd->kd", weights_low, grad_block, preferred_element_type=jnp.float32
        )
        return (
            (key_grad, value_grad),
            query_grad.reshape(rows_block, heads * HEAD_DIM).astype(jnp.bfloat16),
        )

    starts = jnp.arange(total // rows_block, dtype=jnp.int32) * rows_block
    empty = jnp.zeros((total, HEAD_DIM), jnp.float32)
    (key_grad, value_grad), query_grad = lax.scan(one_block, (empty, empty), (starts, logsums))
    return (key_grad, value_grad, query_grad.reshape(total, heads * HEAD_DIM))


def dot_rows(first_operand, second_operand):
    return jnp.einsum(
        "ti,td->id", first_operand, second_operand, preferred_element_type=jnp.float32
    )


def dot_cols(first_operand, second_operand):
    return jnp.einsum(
        "ti,di->td", first_operand, second_operand, preferred_element_type=jnp.float32
    )


def dot(first_operand, second_operand):
    return jnp.dot(first_operand, second_operand, preferred_element_type=jnp.float32)


def low(values):
    return values.astype(jnp.bfloat16)


class Line:
    def __init__(self):
        self.size = lax.axis_size("dp")
        self.length = self.size // 2
        self.place = lax.axis_index("dp")

    def order(self, rank):
        far, step = divmod(rank, self.length)
        return self.place ^ (2 * step + far)

    def rank(self, block):
        offset = block ^ self.place
        return (offset % 2) * self.length + offset // 2

    def pick(self, values, blocks, axis):
        width = values.shape[axis] // self.size
        return jnp.concatenate(
            [lax.dynamic_slice_in_dim(values, block * width, width, axis) for block in blocks], axis
        )

    def inward(self, values, axis=-1):
        axis = axis % values.ndim
        return self.pick(values, [self.order(rank) for rank in range(self.size)], axis)

    def outward(self, values, axis=-1):
        axis = axis % values.ndim
        return self.pick(values, [self.rank(block) for block in range(self.size)], axis)

    def swap(self, values, offset):
        return lax.ppermute(values, "dp", [(i, i ^ offset) for i in range(self.size)])

    def gather_near(self, part):
        return [part] + [self.swap(part, 2 * step) for step in range(1, self.length)]

    def scatter(self, near, far, axis):
        total = near + self.swap(low(far), 1).astype(jnp.float32)
        pieces = jnp.split(total, self.length, axis)
        result = pieces[0]
        for step in range(1, self.length):
            result = result + self.swap(low(pieces[step]), 2 * step).astype(jnp.float32)
        return result


def halves(values, axis=1):
    return jnp.split(values, 2, axis)


def layer(
    tokens,
    cotangent,
    norm1_gain,
    norm1_shift,
    query_weight,
    query_bias,
    keyval_weight,
    value_bias,
    out_weight,
    out_bias,
    norm2_gain,
    norm2_shift,
    fc_weight,
    fc_bias,
    proj_weight,
    proj_bias,
):
    width = tokens.shape[1]
    split = lax.axis_size("tensor")
    position = lax.axis_index("tensor")
    line = Line()
    local_heads = HEADS // split
    query_cols = width // split
    hidden_all = fc_bias.shape[0]
    hidden_cols = hidden_all // split
    own_rows = tokens.shape[0]
    local_qbias = lax.dynamic_slice_in_dim(query_bias, position * query_cols, query_cols)
    local_fbias = lax.dynamic_slice_in_dim(fc_bias, position * hidden_cols, hidden_cols)

    attn_in = jnp.concatenate([query_weight, keyval_weight], axis=1)
    fc_parts, proj_parts = halves(fc_weight, 1), halves(proj_weight, 0)
    pieces_in = line.gather_near(attn_in)
    pieces_out = line.gather_near(out_weight)
    pieces_fc, pieces_proj = [], []
    for i in range(2):
        pieces_fc.append(line.gather_near(fc_parts[i]))
    for i in range(2):
        pieces_proj.append(line.gather_near(proj_parts[i]))
    in_near = jnp.concatenate(pieces_in, axis=0)
    in_far = line.swap(in_near, 1)
    out_near = jnp.concatenate(pieces_out, axis=1)
    out_far = line.swap(out_near, 1)
    fc_near, fc_far, proj_near, proj_far = [], [], [], []
    for i in range(2):
        fc_near.append(jnp.concatenate(pieces_fc[i], axis=0))
        fc_far.append(line.swap(fc_near[i], 1))
    for i in range(2):
        proj_near.append(jnp.concatenate(pieces_proj[i], axis=1))
        proj_far.append(line.swap(proj_near[i], 1))

    residual = line.inward(tokens).astype(jnp.float32)
    own_grad = line.inward(cotangent)
    gain1, shift1, gain2, shift2, bias_out, bias_proj = (
        line.inward(v)
        for v in (norm1_gain, norm1_shift, norm2_gain, norm2_shift, out_bias, proj_bias)
    )

    normed1 = lax.all_gather(
        low(layer_norm(residual, gain1, shift1)), "tensor", axis=0, tiled=True
    )
    out_grad = lax.all_gather(own_grad, "tensor", axis=0, tiled=True)
    normed1_near, normed1_far = halves(normed1)
    in_shift = jnp.concatenate([local_qbias, jnp.zeros((HEAD_DIM,), jnp.float32), value_bias])
    attn_all = low(dot(normed1_near, in_near) + dot(normed1_far, in_far) + in_shift)
    queries, keyval = attn_all[:, :query_cols], attn_all[:, query_cols:]
    attended, logsums, head_peaks = attend_forward(queries, keyval, local_heads)
    attn_terms = jnp.concatenate(
        [low(dot(attended, out_near)), low(dot(attended, out_far))], axis=1
    )
    middle = (
        residual
        + lax.psum_scatter(attn_terms, "tensor", scatter_dimension=0, tiled=True).astype(
            jnp.float32
        )
        + bias_out
    )
    normed2 = lax.all_gather(
        low(layer_norm(middle, gain2, shift2)), "tensor", axis=0, tiled=True
    )
    normed2_near, normed2_far = halves(normed2)
    out_grad_near, out_grad_far = halves(out_grad)

    fbias = halves(local_fbias, 0)
    hidden = []
    for i in range(2):
        hidden.append(
            dot(normed2_near, fc_near[i]) + dot(normed2_far, fc_far[i]) + fbias[i]
        )
    activated = [low(gelu_tanh(h)) for h in hidden]

    proj_sums, hidden_grad = [], []
    for i in range(2):
        proj_sums.append(
            line.scatter(
                dot_rows(activated[i], out_grad_near), dot_rows(activated[i], out_grad_far), 1
            )
        )
        activated_grad = dot_cols(out_grad_near, proj_near[i]) + dot_cols(
            out_grad_far, proj_far[i]
        )
        hidden_grad.append(low(jax.vjp(gelu_tanh, hidden[i])[1](activated_grad)[0]))
    normed2_terms = jnp.concatenate(
        [
            low(sum(dot_cols(hidden_grad[i], weights[i]) for i in range(2)))
            for weights in (fc_near, fc_far)
        ],
        axis=1,
    )
    normed2_grad = lax.psum_scatter(
        normed2_terms, "tensor", scatter_dimension=0, tiled=True
    ).astype(jnp.float32)
    fc_sums = [
        line.scatter(
            dot_rows(normed2_near, hidden_grad[i]), dot_rows(normed2_far, hidden_grad[i]), 0
        )
        for i in range(2)
    ]
    feed_terms = jnp.concatenate(
        [
            low(sum(dot(activated[i], weights[i]) for i in range(2)))
            for weights in (proj_near, proj_far)
        ],
        axis=1,
    )
    mixed = low(
        middle
        + lax.psum_scatter(feed_terms, "tensor", scatter_dimension=0, tiled=True).astype(
            jnp.float32
        )
        + bias_proj
    )

    middle_part, gain2_grad, shift2_grad = jax.vjp(layer_norm, middle, gain2, shift2)[1](
        normed2_grad
    )
    middle_grad = own_grad.astype(jnp.float32) + middle_part
    branch_grad = low(middle_grad)
    branch_rows = lax.all_gather(branch_grad, "tensor", axis=0, tiled=True)
    branch_near, branch_far = halves(branch_rows)
    attended_grad = low(dot_cols(branch_near, out_near) + dot_cols(branch_far, out_far))
    key_grad, value_grad, query_grad = attend_backward(
        queries, keyval, logsums, attended_grad, local_heads
    )
    out_sums = line.scatter(
        dot_rows(attended, branch_near), dot_rows(attended, branch_far), 1
    )
    keyval_grad = lax.psum(low(jnp.concatenate([key_grad, value_grad], axis=1)), "tensor")
    attn_grad = jnp.concatenate([query_grad, keyval_grad], axis=1)
    normed1_terms = jnp.concatenate(
        [
            low(dot_cols(query_grad, weights[:, :query_cols]))
            for weights in (in_near, in_far)
        ],
        axis=1,
    )
    in_sums = line.scatter(
        dot_rows(normed1_near, attn_grad), dot_rows(normed1_far, attn_grad), 0
    )
    keyval_own = lax.dynamic_slice_in_dim(keyval_grad, position * own_rows, own_rows, 0)
    normed1_grad = lax.psum_scatter(
        normed1_terms, "tensor", scatter_dimension=0, tiled=True
    ).astype(jnp.float32)
    normed1_grad = normed1_grad + jnp.concatenate(
        [dot_cols(keyval_own, weights[:, query_cols:]) for weights in (in_near, in_far)], axis=1
    )
    residual_part, gain1_grad, shift1_grad = jax.vjp(layer_norm, residual, gain1, shift1)[1](
        normed1_grad
    )
    token_grad = low(middle_grad + residual_part)

    count = line.size * split
    slots = lax.dynamic_update_slice_in_dim(
        jnp.zeros((count * local_heads,), jnp.float32),
        head_peaks,
        (line.place * split + position) * local_heads,
        0,
    )
    fc_bias_part = lax.dynamic_update_slice_in_dim(
        jnp.zeros((hidden_all,), jnp.float32),
        jnp.concatenate([jnp.sum(h, axis=0, dtype=jnp.float32) for h in hidden_grad]),
        position * hidden_cols,
        0,
    )
    early = [
        line.outward(gain2_grad),
        line.outward(shift2_grad),
        line.outward(jnp.sum(branch_grad, axis=0, dtype=jnp.float32)),
        line.outward(jnp.sum(own_grad, axis=0, dtype=jnp.float32)),
        fc_bias_part,
        slots,
    ]
    query_bias_part = lax.dynamic_update_slice_in_dim(
        jnp.zeros((width,), jnp.float32),
        jnp.sum(query_grad, axis=0, dtype=jnp.float32),
        position * query_cols,
        0,
    )
    late = [
        line.outward(gain1_grad),
        line.outward(shift1_grad),
        query_bias_part,
        jnp.sum(keyval_own[:, HEAD_DIM:], axis=0, dtype=jnp.float32),
    ]

    parts = early + late
    sizes = [part.shape[0] for part in parts]
    whole = jnp.concatenate(parts)
    moved = [
        lax.ppermute(whole, "tensor", [(i, i ^ step) for i in range(split)])
        for step in range(1, split)
    ]
    whole = sum(moved, whole)
    whole = whole + line.swap(whole, 1)
    moved = [line.swap(whole, 2 * step) for step in range(1, line.length)]
    whole = sum(moved, whole)
    ends = [sum(sizes[: i + 1]) for i in range(len(sizes) - 1)]
    (
        gain2_sum,
        shift2_sum,
        out_bias_sum,
        proj_bias_sum,
        fc_bias_sum,
        slot_sum,
        gain1_sum,
        shift1_sum,
        query_bias_sum,
        value_bias_sum,
    ) = jnp.split(whole, ends)

    peaks = jnp.max(slot_sum.reshape(line.size, HEADS), axis=0)
    clip_factor = CLIP_LIMIT / jnp.maximum(peaks, CLIP_LIMIT)
    key_factor = jnp.sqrt(jnp.min(clip_factor))
    local_clip = lax.dynamic_slice_in_dim(clip_factor, position * local_heads, local_heads)
    column_factor = jnp.repeat(local_clip / key_factor, HEAD_DIM)
    clipped_query = low(query_weight.astype(jnp.float32) * column_factor[None, :])
    clipped_key = low(keyval_weight[:, :HEAD_DIM].astype(jnp.float32) * key_factor)
    return (
        line.outward(mixed),
        line.outward(token_grad),
        gain1_sum,
        shift1_sum,
        in_sums[:, :query_cols],
        query_bias_sum,
        in_sums[:, query_cols:],
        value_bias_sum,
        out_sums,
        out_bias_sum,
        gain2_sum,
        shift2_sum,
        jnp.concatenate(fc_sums, axis=1),
        fc_bias_sum,
        jnp.concatenate(proj_sums, axis=0),
        proj_bias_sum,
        clipped_query,
        clipped_key,
    )


def solution(mesh):
    return jax.shard_map(
        layer,
        mesh=mesh,
        in_specs=(
            P(("dp", "tensor"), None),
            P(("dp", "tensor"), None),
            P(),
            P(),
            P("dp", "tensor"),
            P(),
            P("dp", None),
            P(),
            P("tensor", "dp"),
            P(),
            P(),
            P(),
            P("dp", "tensor"),
            P(),
            P("tensor", "dp"),
            P(),
        ),
        out_specs=(
            P(("dp", "tensor"), None),
            P(("dp", "tensor"), None),
            P(),
            P(),
            P("dp", "tensor"),
            P(),
            P("dp", None),
            P(),
            P("tensor", "dp"),
            P(),
            P(),
            P(),
            P("dp", "tensor"),
            P(),
            P("tensor", "dp"),
            P(),
            P("dp", "tensor"),
            P("dp", None),
        ),
        check_vma=False,
    )
```

time: 1540 us -> 1070 us (0.69)
  waiting for transfers between devices: 1180 us -> 607 us
  starting transfers between devices: 1.45 us -> 72.7 us
  blocking collectives: 40.4 us -> 0 us
  matrix products: 176 us -> 210 us
  other arithmetic: 63.5 us -> 83 us
  local copies, waits for them, and re-layouts: 39.8 us -> 56.7 us
    ppermute x0 -> x55, waiting for transfers between devices: none -> 500 us  [the longest x52 496 us: swap(): lax.ppermute(values, 'dp', [(i, i ^ offset) for i in range(self.size)])]
    reduce_scatter x9 -> x4, waiting for transfers between devices: 588 us -> 107 us  [the longest x1 41.7 us: layer(): lax.psum_scatter(feed_terms, 'tensor', scatter_dimension=0, tiled=True)]
    all_gather x9 -> x4, waiting for transfers between devices: 456 us -> 0.01 us  [the longest x1 0.01 us: layer(): lax.all_gather(low(layer_norm(residual, gain1, shift1)), 'tensor', axis=0...]
    psum x2 -> x1, waiting for transfers between devices: 134 us -> 0.01 us  [layer(): lax.psum(low(jnp.concatenate([key_grad, value_grad], axis=1)), 'tensor')]
    ppermute x0 -> x55, starting transfers between devices: none -> 71.3 us  [the longest x52 69.4 us: swap(): lax.ppermute(values, 'dp', [(i, i ^ offset) for i in range(self.size)])]
    pmax x1 -> x0, blocking collectives: 40.4 us -> none  [per_device(): peak_table = lax.pmax(peak_table, ('dp', 'tensor'))]
    concatenate x0 -> x13, other arithmetic: none -> 20.3 us  [the longest x2 4.51 us: layer(): fc_near.append(jnp.concatenate(pieces_fc[i], axis=0))]
    dot_general x15 -> x38, matrix products: 142 us -> 153 us  [the longest x14 54.8 us: dot_cols(): jnp.einsum('ti,di->td', first_operand, second_operand, preferred_element_...]
  transfers between devices with their start and end apart: 20 -> 64, of which waited for: 18 -> 37; matrix products, arithmetic and copies ran while one was open for 11% -> 26% of each run, Pallas kernels for 0% -> 0%
where the time goes in v1:
time: 1070 us; the launch traced here: 1060 us
  waiting for transfers between devices  607 us (57%)
  matrix products  210 us (20%)
  other arithmetic  83 us (8%)
  starting transfers between devices  72.7 us (7%)
  local copies, waits for them, and re-layouts  56.7 us (5%)
  between operations  16.9 us (2%)
    ppermute x52, waiting for transfers between devices, swap(): lax.ppermute(values, 'dp', [(i, i ^ offset) for i in range(self.size)])  496 us
    ppermute x52, starting transfers between devices, swap(): lax.ppermute(values, 'dp', [(i, i ^ offset) for i in range(self.size)])  69.4 us
    dot_general x14, matrix products, dot_cols(): jnp.einsum('ti,di->td', first_operand, second_operand, preferred_element_...  54.8 us
    dot_general x12, matrix products, dot(): jnp.dot(first_operand, second_operand, preferred_element_type=jnp.float32)  52 us
    dot_general x12, matrix products, dot_rows(): jnp.einsum('ti,td->id', first_operand, second_operand, preferred_element_...  45.8 us
    reduce_scatter x1, waiting for transfers between devices, layer(): lax.psum_scatter(feed_terms, 'tensor', scatter_dimension=0, tiled=True)  41.7 us
    reduce_scatter x1, waiting for transfers between devices, layer(): lax.psum_scatter(attn_terms, 'tensor', scatter_dimension=0, tiled=True)  41.3 us
    reduce_scatter x1, waiting for transfers between devices, layer(): lax.psum_scatter(normed2_terms, 'tensor', scatter_dimension=0, tiled=True)  24.3 us
  transfers between devices with their start and end apart: 64, of which 37 were waited for; matrix products, arithmetic and copies ran while one was open for 26% of the time, Pallas kernels for 0%

profile of v1, /device:TPU:8, one launch (start us, length us, event | category | flops | bytes accessed | tf_op | source)
XLA Modules:
  0.0 1055.2 jit_solution(7499077474124067253)
XLA Ops:
  17.5 24.6 %collective-permute-done.2 = bf16[256,768]{1,0:T(8,128)(2,1)S(1)} collective-permute-done((bf16[256,768]{1,0:T(8,128)(2,1)S(1)}, bf16[256,768]{1,0:T(8,128)(2,1)S(1)}, u32[]{:S(2)}, u32[]{:S(2)}) %collective-permute-start.2) | collective-permute-done | bytes 393248 | tf_op jit(solution)/shard_map/ppermute | solution.py:166
  42.1 6.6 collective-permute-done.1
  58.6 4.8 collective-permute-done.4
  65.1 8.1 collective-permute-done.5
  80.0 7.5 collective-permute-done.3
  87.5 4.1 fusion.106
  96.4 40.6 %while.35 = (s32[]{:T(128)}, bf16[2,512,512]{2,1,0:T(8,128)(2,1)}, f32[2,4,512]{2,1,0:T(4,128)S(1)}, f32[2,4]{1,0:T(2,128)S(1)}, s32[2]{0:T(128)S(1)}, /*index=5...) while((s32[]{:T(128)}, bf16[2,512,512]{2,1,0:T(8,128)(2,1)}, ...), condition=%wide.region_6.7_spmd, body=%wide.region_2.6_spmd.sunk | while | flops 1107077632 | bytes 76636472 | solution.py:67
  111.5 5.1 fusion.280
  131.8 5.1 fusion.280
  150.7 41.3 %reduce-scatter.5.cloned.1.call-done = bf16[256,2048]{0,1:T(8,128)(2,1)} async-done(((bf16[1024,2048]{0,1:T(8,128)(2,1)}), bf16[256,2048]{0,1:T(8,128)(2,1)}) %reduce-scatter.5.cloned.1.call-update) | async-done | bytes 1048592 | tf_op jit(solution)/shard_map/reduce_scatter | solution.py:256
  205.1 30.9 %collective-permute-done.21 = bf16[1024,256]{1,0:T(8,128)(2,1)S(1)} collective-permute-done((bf16[1024,256]{1,0:T(8,128)(2,1)S(1)}, bf16[1024,256]{1,0:T(8,128)(2,1)S(1)}, u32[]{:S(2)}, u32[]{:S(2)}) %collective-permute-start.21) | collective-permute-done | bytes 524320 | tf_op jit(solution)/shard_map/ppermute | solution.py:166
  236.0 31.8 %collective-permute-done.20 = bf16[1024,256]{1,0:T(8,128)(2,1)S(1)} collective-permute-done((bf16[1024,256]{1,0:T(8,128)(2,1)S(1)}, bf16[1024,256]{1,0:T(8,128)(2,1)S(1)}, u32[]{:S(2)}, u32[]{:S(2)}) %collective-permute-start.20) | collective-permute-done | bytes 524320 | tf_op jit(solution)/shard_map/ppermute | solution.py:166
  272.1 18.8 %collective-permute-done.14 = bf16[1024,256]{1,0:T(8,128)(2,1)S(1)} collective-permute-done((bf16[1024,256]{1,0:T(8,128)(2,1)S(1)}, bf16[1024,256]{1,0:T(8,128)(2,1)S(1)}, u32[]{:S(2)}, u32[]{:S(2)}) %collective-permute-start.14) | collective-permute-done | bytes 524320 | tf_op jit(solution)/shard_map/ppermute | solution.py:166
  291.0 21.8 %collective-permute-done.13 = bf16[1024,256]{1,0:T(8,128)(2,1)S(1)} collective-permute-done((bf16[1024,256]{1,0:T(8,128)(2,1)S(1)}, bf16[1024,256]{1,0:T(8,128)(2,1)S(1)}, u32[]{:S(2)}, u32[]{:S(2)}) %collective-permute-start.13) | collective-permute-done | bytes 524320 | tf_op jit(solution)/shard_map/ppermute | solution.py:166
  318.1 8.6 collective-permute-done.17
  328.8 17.7 %collective-permute-done.16 = bf16[256,1024]{1,0:T(8,128)(2,1)S(1)} collective-permute-done((bf16[256,1024]{1,0:T(8,128)(2,1)S(1)}, bf16[256,1024]{1,0:T(8,128)(2,1)S(1)}, u32[]{:S(2)}, u32[]{:S(2)}) %collective-permute-start.16) | collective-permute-done | bytes 524320 | tf_op jit(solution)/shard_map/ppermute | solution.py:166
  353.0 16.7 %collective-permute-done.10 = bf16[256,1024]{1,0:T(8,128)(2,1)} collective-permute-done((bf16[256,1024]{1,0:T(8,128)(2,1)}, bf16[256,1024]{1,0:T(8,128)(2,1)}, u32[]{:S(2)}, u32[]{:S(2)}) %collective-permute-start.10) | collective-permute-done | bytes 524320 | tf_op jit(solution)/shard_map/ppermute | solution.py:166
  370.4 8.6 collective-permute-done.9
  379.0 11.1 %collective-permute-done.8 = bf16[256,1024]{1,0:T(8,128)(2,1)} collective-permute-done((bf16[256,1024]{1,0:T(8,128)(2,1)}, bf16[256,1024]{1,0:T(8,128)(2,1)}, u32[]{:S(2)}, u32[]{:S(2)}) %collective-permute-start.8) | collective-permute-done | bytes 524320 | tf_op jit(solution)/shard_map/ppermute | solution.py:166
  394.7 6.8 fusion.128
  401.5 6.0 fusion.130
  410.4 4.8 fusion.144
  415.3 5.1 multiply_convert_fusion
  420.5 5.8 convert_reduce_fusion
  428.8 4.0 fusion.213
  432.7 19.6 %collective-permute-done.11 = bf16[1024,1024]{1,0:T(8,128)(2,1)} collective-permute-done((bf16[1024,1024]{1,0:T(8,128)(2,1)}, bf16[1024,1024]{1,0:T(8,128)(2,1)}, u32[]{:S(2)}, u32[]{:S(2)}) %collective-permute-start.11) | collective-permute-done | bytes 2097184 | tf_op jit(solution)/shard_map/ppermute | solution.py:166
  452.3 6.0 fusion.146
  458.3 9.3 multiply_convert_fusion.1
  467.6 7.6 convert_reduce_fusion.1
  475.3 4.8 add_convert_fusion
  480.1 3.9 add_convert_fusion.1
  486.9 4.5 fusion.190
  491.5 4.2 fusion.212
  498.1 4.0 add_convert_fusion.2
  505.5 24.3 %reduce-scatter.9.cloned.1.call-done = bf16[256,2048]{0,1:T(8,128)(2,1)} async-done(((bf16[1024,2048]{0,1:T(8,128)(2,1)}), bf16[256,2048]{0,1:T(8,128)(2,1)}) %reduce-scatter.9.cloned.1.call-update) | async-done | bytes 1048592 | tf_op jit(solution)/shard_map/reduce_scatter | solution.py:293
  534.8 41.7 %reduce-scatter.7.cloned.1.call-done = bf16[256,2048]{0,1:T(8,128)(2,1)} async-done(((bf16[1024,2048]{0,1:T(8,128)(2,1)}), bf16[256,2048]{0,1:T(8,128)(2,1)}) %reduce-scatter.7.cloned.1.call-update) | async-done | bytes 1048592 | tf_op jit(solution)/shard_map/reduce_scatter | solution.py:311
  576.6 4.3 convert_reduce_fusion.6
  581.0 5.9 convolution_convert_fusion.2
  588.8 5.2 convolution_convert_fusion.3
  602.4 33.2 %collective-permute-done.43 = bf16[1024,1024]{0,1:T(8,128)(2,1)S(1)} collective-permute-done((bf16[1024,1024]{0,1:T(8,128)(2,1)}, bf16[1024,1024]{0,1:T(8,128)(2,1)S(1)}, u32[]{:S(2)}, u32[]{:S(2)}) %collective-permute-start.43) | collective-permute-done | bytes 2097184 | tf_op jit(solution)/shard_map/ppermute | solution.py:166
  641.3 39.3 %collective-permute-done.39 = bf16[1024,1024]{0,1:T(8,128)(2,1)S(1)} collective-permute-done((bf16[1024,1024]{0,1:T(8,128)(2,1)S(1)}, bf16[1024,1024]{0,1:T(8,128)(2,1)S(1)}, u32[]{:S(2)}, u32[]{:S(2)}) %collective-permute-start.39) | collective-permute-done | bytes 2097184 | tf_op jit(solution)/shard_map/ppermute | solution.py:166
  681.1 5.0 fusion.209
  687.3 38.2 %collective-permute-done.51 = bf16[1024,1024]{1,0:T(8,128)(2,1)S(1)} collective-permute-done((bf16[1024,1024]{1,0:T(8,128)(2,1)S(1)}, bf16[1024,1024]{1,0:T(8,128)(2,1)S(1)}, u32[]{:S(2)}, u32[]{:S(2)}) %collective-permute-start.51) | collective-permute-done | bytes 2097184 | tf_op jit(solution)/shard_map/ppermute | solution.py:166
  727.0 4.5 fusion.210
  731.5 37.6 %collective-permute-done.47 = bf16[1024,1024]{1,0:T(8,128)(2,1)S(1)} collective-permute-done((bf16[1024,1024]{1,0:T(8,128)(2,1)S(1)}, bf16[1024,1024]{1,0:T(8,128)(2,1)S(1)}, u32[]{:S(2)}, u32[]{:S(2)}) %collective-permute-start.47) | collective-permute-done | bytes 2097184 | tf_op jit(solution)/shard_map/ppermute | solution.py:166
  771.6 4.5 fusion.211
  789.9 65.5 %while.36 = (s32[]{:T(128)}, f32[1024,128]{1,0:T(8,128)}, f32[1024,128]{1,0:T(8,128)}, bf16[2,512,512]{1,2,0:T(8,128)(2,1)}, s32[2]{0:T(128)S(1)}, /*index=5*/bf...) while((s32[]{:T(128)}, f32[1024,128]{1,0:T(8,128)}, ...), condition=%wide.region_16.17_spmd.clone, body=%wide.region_14.16_spmd.clone.sunk | while | flops 2718607872 | bytes 139805232 | solution.py:113
  792.9 4.7 fusion.290
  799.2 6.0 fusion.291
  812.7 6.2 fusion.294
  825.6 4.7 fusion.290
  831.8 6.0 fusion.291
  845.4 6.2 fusion.294
  876.3 16.5 %collective-permute-done.52 = bf16[1024,256]{1,0:T(8,128)(2,1)} collective-permute-done((bf16[1024,256]{1,0:T(8,128)(2,1)}, bf16[1024,256]{1,0:T(8,128)(2,1)}, u32[]{:S(2)}, u32[]{:S(2)}) %collective-permute-start.52) | collective-permute-done | bytes 524320 | tf_op jit(solution)/shard_map/ppermute | solution.py:166
  894.7 10.9 %collective-permute-done.50 = bf16[1024,256]{1,0:T(8,128)(2,1)} collective-permute-done((bf16[1024,256]{1,0:T(8,128)(2,1)}, bf16[1024,256]{1,0:T(8,128)(2,1)}, u32[]{:S(2)}, u32[]{:S(2)}) %collective-permute-start.50) | collective-permute-done | bytes 524320 | tf_op jit(solution)/shard_map/ppermute | solution.py:166
  905.6 6.0 collective-permute-done.49
  922.7 4.7 fusion.114
  931.9 15.6 %collective-permute-done.35 = bf16[512,1024]{1,0:T(8,128)(2,1)} collective-permute-done((bf16[512,1024]{1,0:T(8,128)(2,1)}, bf16[512,1024]{1,0:T(8,128)(2,1)}, u32[]{:S(2)}, u32[]{:S(2)}) %collective-permute-start.35) | collective-permute-done | bytes 1048608 | tf_op jit(solution)/shard_map/ppermute | solution.py:166
  950.8 3.9 collective-permute-start.37
  954.7 22.8 %collective-permute-done.31 = bf16[1024,768]{1,0:T(8,128)(2,1)} collective-permute-done((bf16[1024,768]{1,0:T(8,128)(2,1)}, bf16[1024,768]{1,0:T(8,128)(2,1)}, u32[]{:S(2)}, u32[]{:S(2)}) %collective-permute-start.31) | collective-permute-done | bytes 1572896 | tf_op jit(solution)/shard_map/ppermute | solution.py:166
  980.8 3.8 collective-permute-start.33
  987.0 19.9 %collective-permute-done.34 = bf16[256,768]{1,0:T(8,128)(2,1)S(1)} collective-permute-done((bf16[256,768]{1,0:T(8,128)(2,1)S(1)}, bf16[256,768]{1,0:T(8,128)(2,1)S(1)}, u32[]{:S(2)}, u32[]{:S(2)}) %collective-permute-start.34) | collective-permute-done | bytes 393248 | tf_op jit(solution)/shard_map/ppermute | solution.py:166
  1007.0 4.3 collective-permute-done.33
  1034.4 4.3 collective-permute-start.29
  (724 shorter events, 270.0 us)
Async XLA Ops:
  7.2 80.3 %all-gather.5.cloned.1.call-start = ((), (), s32[]{:S(2)}) async-start(), calls=%async_computation.4 | async-start | bytes 5242880 | tf_op jit(solution)/shard_map/all_gather | solution.py:242
  13.2 178.8 %reduce-scatter.5.cloned.1.call-start = ((), (), s32[]{:S(2)}) async-start(), calls=%async_computation.5 | async-start | bytes 5242880 | tf_op jit(solution)/shard_map/reduce_scatter | solution.py:256
  13.3 28.7 %collective-permute-start.2 = (bf16[256,768]{1,0:T(8,128)(2,1)S(1)}, bf16[256,768]{1,0:T(8,128)(2,1)S(1)}, u32[]{:S(2)}, u32[]{:S(2)}) collective-permute-start(bf16[256,768]{1,0:T(8,128)(2,1)S(1)} %constant_dynamic-update-slice_fusion.11), channel_id=1, source_target_pairs={{0,24},{4,28},{8,16},{12,20},{16,8},{20,12},{24,0},{28,4},{1,25},{... | collective-permute-start | bytes 1179656 | tf_op jit(solution)/shard_map/ppermute | solution.py:166
  15.0 33.7 %collective-permute-start.1 = (bf16[256,768]{1,0:T(8,128)(2,1)S(1)}, bf16[256,768]{1,0:T(8,128)(2,1)S(1)}, u32[]{:S(2)}, u32[]{:S(2)}) collective-permute-start(bf16[256,768]{1,0:T(8,128)(2,1)S(1)} %constant_dynamic-update-slice_fusion.11), channel_id=1, source_target_pairs={{0,16},{4,20},{8,24},{12,28},{16,0},{20,4},{24,8},{28,12},{1,17},{... | collective-permute-start | bytes 1179656 | tf_op jit(solution)/shard_map/ppermute | solution.py:166
  16.1 32.6 %collective-permute-start = (bf16[256,768]{1,0:T(8,128)(2,1)S(1)}, bf16[256,768]{1,0:T(8,128)(2,1)S(1)}, u32[]{:S(2)}, u32[]{:S(2)}) collective-permute-start(bf16[256,768]{1,0:T(8,128)(2,1)S(1)} %constant_dynamic-update-slice_fusion.11), channel_id=1, source_target_pairs={{0,8},{4,12},{8,0},{12,4},{16,24},{20,28},{24,16},{28,20},{1,9},{5... | collective-permute-start | bytes 1179656 | tf_op jit(solution)/shard_map/ppermute | solution.py:166
  50.1 37.4 %collective-permute-start.3 = (bf16[1024,768]{1,0:T(8,128)(2,1)S(1)}, bf16[1024,768]{1,0:T(8,128)(2,1)}, u32[]{:S(2)}, u32[]{:S(2)}) collective-permute-start(bf16[1024,768]{1,0:T(8,128)(2,1)S(1)} %pad_maximum_fusion.10), channel_id=1, source_target_pairs={{0,4},{4,0},{8,12},{12,8},{16,20},{20,16},{24,28},{28,24},{1,5},{5... | collective-permute-start | bytes 4718600 | tf_op jit(solution)/shard_map/ppermute | solution.py:166
  51.6 11.8 %collective-permute-start.4 = (bf16[512,256]{1,0:T(8,128)(2,1)}, bf16[512,256]{1,0:T(8,128)(2,1)}, u32[]{:S(2)}, u32[]{:S(2)}) collective-permute-start(bf16[512,256]{1,0:T(8,128)(2,1)} %param.28), channel_id=1, source_target_pairs={{0,8},{4,12},{8,0},{12,4},{16,24},{20,28},{24,16},{28,20},{1,9},{5... | collective-permute-start | bytes 786440 | tf_op jit(solution)/shard_map/ppermute | solution.py:166
  54.0 19.3 %collective-permute-start.5 = (bf16[512,256]{1,0:T(8,128)(2,1)}, bf16[512,256]{1,0:T(8,128)(2,1)}, u32[]{:S(2)}, u32[]{:S(2)}) collective-permute-start(bf16[512,256]{1,0:T(8,128)(2,1)} %param.28), channel_id=1, source_target_pairs={{0,16},{4,20},{8,24},{12,28},{16,0},{20,4},{24,8},{28,12},{1,17},{... | collective-permute-start | bytes 786440 | tf_op jit(solution)/shard_map/ppermute | solution.py:166
  55.0 22.7 %collective-permute-start.6 = (bf16[512,256]{1,0:T(8,128)(2,1)}, bf16[512,256]{1,0:T(8,128)(2,1)}, u32[]{:S(2)}, u32[]{:S(2)}) collective-permute-start(bf16[512,256]{1,0:T(8,128)(2,1)} %param.28), channel_id=1, source_target_pairs={{0,24},{4,28},{8,16},{12,20},{16,8},{20,12},{24,0},{28,4},{1,25},{... | collective-permute-start | bytes 786440 | tf_op jit(solution)/shard_map/ppermute | solution.py:166
  79.5 60.9 %collective-permute-start.7 = (bf16[512,1024]{1,0:T(8,128)(2,1)}, bf16[512,1024]{1,0:T(8,128)(2,1)}, u32[]{:S(2)}, u32[]{:S(2)}) collective-permute-start(bf16[512,1024]{1,0:T(8,128)(2,1)} %constant_dynamic-update-slice_fusion.13), channel_id=1, source_target_pairs={{0,4},{4,0},{8,12},{12,8},{16,20},{20,16},{24,28},{28,24},{1,5},{5... | collective-permute-start | bytes 3145736 | tf_op jit(solution)/shard_map/ppermute | solution.py:166
  145.4 249.3 %all-gather.9.cloned.1.call-start = ((), (), s32[]{:S(2)}) async-start(), calls=%async_computation.8 | async-start | bytes 5242880 | tf_op jit(solution)/shard_map/all_gather | solution.py:245
  148.8 261.6 %all-gather.7.cloned.1.call-start = ((), (), s32[]{:S(2)}) async-start(), calls=%async_computation.6 | async-start | bytes 5242880 | tf_op jit(solution)/shard_map/all_gather | solution.py:261
  196.1 333.7 %reduce-scatter.9.cloned.1.call-start = ((), (), s32[]{:S(2)}) async-start(), calls=%async_computation.9 | async-start | bytes 5242880 | tf_op jit(solution)/shard_map/reduce_scatter | solution.py:293
  197.8 38.2 %collective-permute-start.21 = (bf16[1024,256]{1,0:T(8,128)(2,1)S(1)}, bf16[1024,256]{1,0:T(8,128)(2,1)S(1)}, u32[]{:S(2)}, u32[]{:S(2)}) collective-permute-start(bf16[1024,256]{1,0:T(8,128)(2,1)S(1)} %get-tuple-element.526), channel_id=1, source_target_pairs={{0,24},{4,28},{8,16},{12,20},{16,8},{20,12},{24,0},{28,4},{1,25},{... | collective-permute-start | bytes 1572872 | tf_op jit(solution)/shard_map/ppermute | solution.py:166
  199.3 68.5 %collective-permute-start.20 = (bf16[1024,256]{1,0:T(8,128)(2,1)S(1)}, bf16[1024,256]{1,0:T(8,128)(2,1)S(1)}, u32[]{:S(2)}, u32[]{:S(2)}) collective-permute-start(bf16[1024,256]{1,0:T(8,128)(2,1)S(1)} %get-tuple-element.526), channel_id=1, source_target_pairs={{0,16},{4,20},{8,24},{12,28},{16,0},{20,4},{24,8},{28,12},{1,17},{... | collective-permute-start | bytes 1572872 | tf_op jit(solution)/shard_map/ppermute | solution.py:166
  200.7 67.1 %collective-permute-start.19 = (bf16[1024,256]{1,0:T(8,128)(2,1)S(1)}, bf16[1024,256]{1,0:T(8,128)(2,1)S(1)}, u32[]{:S(2)}, u32[]{:S(2)}) collective-permute-start(bf16[1024,256]{1,0:T(8,128)(2,1)S(1)} %get-tuple-element.526), channel_id=1, source_target_pairs={{0,8},{4,12},{8,0},{12,4},{16,24},{20,28},{24,16},{28,20},{1,9},{5... | collective-permute-start | bytes 1572872 | tf_op jit(solution)/shard_map/ppermute | solution.py:166
  201.7 89.3 %collective-permute-start.14 = (bf16[1024,256]{1,0:T(8,128)(2,1)S(1)}, bf16[1024,256]{1,0:T(8,128)(2,1)S(1)}, u32[]{:S(2)}, u32[]{:S(2)}) collective-permute-start(bf16[1024,256]{1,0:T(8,128)(2,1)S(1)} %get-tuple-element.525), channel_id=1, source_target_pairs={{0,24},{4,28},{8,16},{12,20},{16,8},{20,12},{24,0},{28,4},{1,25},{... | collective-permute-start | bytes 1572872 | tf_op jit(solution)/shard_map/ppermute | solution.py:166
  203.2 109.6 %collective-permute-start.13 = (bf16[1024,256]{1,0:T(8,128)(2,1)S(1)}, bf16[1024,256]{1,0:T(8,128)(2,1)S(1)}, u32[]{:S(2)}, u32[]{:S(2)}) collective-permute-start(bf16[1024,256]{1,0:T(8,128)(2,1)S(1)} %get-tuple-element.525), channel_id=1, source_target_pairs={{0,16},{4,20},{8,24},{12,28},{16,0},{20,4},{24,8},{28,12},{1,17},{... | collective-permute-start | bytes 1572872 | tf_op jit(solution)/shard_map/ppermute | solution.py:166
  236.0 78.9 %collective-permute-start.12 = (bf16[1024,256]{1,0:T(8,128)(2,1)S(1)}, bf16[1024,256]{1,0:T(8,128)(2,1)S(1)}, u32[]{:S(2)}, u32[]{:S(2)}) collective-permute-start(bf16[1024,256]{1,0:T(8,128)(2,1)S(1)} %get-tuple-element.525), channel_id=1, source_target_pairs={{0,8},{4,12},{8,0},{12,4},{16,24},{20,28},{24,16},{28,20},{1,9},{5... | collective-permute-start | bytes 1572872 | tf_op jit(solution)/shard_map/ppermute | solution.py:166
  269.5 125.2 %collective-permute-start.23 = (bf16[1024,1024]{1,0:T(8,128)(2,1)}, bf16[1024,1024]{1,0:T(8,128)(2,1)}, u32[]{:S(2)}, u32[]{:S(2)}) collective-permute-start(bf16[1024,1024]{1,0:T(8,128)(2,1)} %pad_maximum_fusion.7), channel_id=1, source_target_pairs={{0,4},{4,0},{8,12},{12,8},{16,20},{20,16},{24,28},{28,24},{1,5},{5... | collective-permute-start | bytes 6291464 | tf_op jit(solution)/shard_map/ppermute | solution.py:166
  271.9 54.9 %collective-permute-start.17 = (bf16[256,1024]{1,0:T(8,128)(2,1)S(1)}, bf16[256,1024]{1,0:T(8,128)(2,1)S(1)}, u32[]{:S(2)}, u32[]{:S(2)}) collective-permute-start(bf16[256,1024]{1,0:T(8,128)(2,1)S(1)} %get-tuple-element.528), channel_id=1, source_target_pairs={{0,24},{4,28},{8,16},{12,20},{16,8},{20,12},{24,0},{28,4},{1,25},{... | collective-permute-start | bytes 1572872 | tf_op jit(solution)/shard_map/ppermute | solution.py:166
  291.0 55.5 %collective-permute-start.16 = (bf16[256,1024]{1,0:T(8,128)(2,1)S(1)}, bf16[256,1024]{1,0:T(8,128)(2,1)S(1)}, u32[]{:S(2)}, u32[]{:S(2)}) collective-permute-start(bf16[256,1024]{1,0:T(8,128)(2,1)S(1)} %get-tuple-element.528), channel_id=1, source_target_pairs={{0,16},{4,20},{8,24},{12,28},{16,0},{20,4},{24,8},{28,12},{1,17},{... | collective-permute-start | bytes 1572872 | tf_op jit(solution)/shard_map/ppermute | solution.py:166
  312.8 34.1 %collective-permute-start.15 = (bf16[256,1024]{1,0:T(8,128)(2,1)S(1)}, bf16[256,1024]{1,0:T(8,128)(2,1)S(1)}, u32[]{:S(2)}, u32[]{:S(2)}) collective-permute-start(bf16[256,1024]{1,0:T(8,128)(2,1)S(1)} %get-tuple-element.528), channel_id=1, source_target_pairs={{0,8},{4,12},{8,0},{12,4},{16,24},{20,28},{24,16},{28,20},{1,9},{5... | collective-permute-start | bytes 1572872 | tf_op jit(solution)/shard_map/ppermute | solution.py:166
  316.6 84.9 %collective-permute-start.22 = (bf16[1024,1024]{1,0:T(8,128)(2,1)}, bf16[1024,1024]{1,0:T(8,128)(2,1)}, u32[]{:S(2)}, u32[]{:S(2)}) collective-permute-start(bf16[1024,1024]{1,0:T(8,128)(2,1)} %pad_maximum_fusion.5), channel_id=1, source_target_pairs={{0,4},{4,0},{8,12},{12,8},{16,20},{20,16},{24,28},{28,24},{1,5},{5... | collective-permute-start | bytes 6291464 | tf_op jit(solution)/shard_map/ppermute | solution.py:166
  326.7 43.0 %collective-permute-start.10 = (bf16[256,1024]{1,0:T(8,128)(2,1)}, bf16[256,1024]{1,0:T(8,128)(2,1)}, u32[]{:S(2)}, u32[]{:S(2)}) collective-permute-start(bf16[256,1024]{1,0:T(8,128)(2,1)} %get-tuple-element.527), channel_id=1, source_target_pairs={{0,24},{4,28},{8,16},{12,20},{16,8},{20,12},{24,0},{28,4},{1,25},{... | collective-permute-start | bytes 1572872 | tf_op jit(solution)/shard_map/ppermute | solution.py:166
  348.4 62.0 %collective-permute-start.18 = (bf16[1024,1024]{1,0:T(8,128)(2,1)}, bf16[1024,1024]{1,0:T(8,128)(2,1)}, u32[]{:S(2)}, u32[]{:S(2)}) collective-permute-start(bf16[1024,1024]{1,0:T(8,128)(2,1)} %pad_maximum_fusion.6), channel_id=1, source_target_pairs={{0,4},{4,0},{8,12},{12,8},{16,20},{20,16},{24,28},{28,24},{1,5},{5... | collective-permute-start | bytes 6291464 | tf_op jit(solution)/shard_map/ppermute | solution.py:166
  349.9 29.1 %collective-permute-start.9 = (bf16[256,1024]{1,0:T(8,128)(2,1)}, bf16[256,1024]{1,0:T(8,128)(2,1)}, u32[]{:S(2)}, u32[]{:S(2)}) collective-permute-start(bf16[256,1024]{1,0:T(8,128)(2,1)} %get-tuple-element.527), channel_id=1, source_target_pairs={{0,16},{4,20},{8,24},{12,28},{16,0},{20,4},{24,8},{28,12},{1,17},{... | collective-permute-start | bytes 1572872 | tf_op jit(solution)/shard_map/ppermute | solution.py:166
  369.7 20.4 %collective-permute-start.8 = (bf16[256,1024]{1,0:T(8,128)(2,1)}, bf16[256,1024]{1,0:T(8,128)(2,1)}, u32[]{:S(2)}, u32[]{:S(2)}) collective-permute-start(bf16[256,1024]{1,0:T(8,128)(2,1)} %get-tuple-element.527), channel_id=1, source_target_pairs={{0,8},{4,12},{8,0},{12,4},{16,24},{20,28},{24,16},{28,20},{1,9},{5... | collective-permute-start | bytes 1572872 | tf_op jit(solution)/shard_map/ppermute | solution.py:166
  393.2 59.1 %collective-permute-start.11 = (bf16[1024,1024]{1,0:T(8,128)(2,1)}, bf16[1024,1024]{1,0:T(8,128)(2,1)}, u32[]{:S(2)}, u32[]{:S(2)}) collective-permute-start(bf16[1024,1024]{1,0:T(8,128)(2,1)} %pad_maximum_fusion.4), channel_id=1, source_target_pairs={{0,4},{4,0},{8,12},{12,8},{16,20},{20,16},{24,28},{28,24},{1,5},{5... | collective-permute-start | bytes 6291464 | tf_op jit(solution)/shard_map/ppermute | solution.py:166
  486.4 90.1 %reduce-scatter.7.cloned.1.call-start = ((), (), s32[]{:S(2)}) async-start(), calls=%async_computation.7 | async-start | bytes 5242880 | tf_op jit(solution)/shard_map/reduce_scatter | solution.py:311
  504.7 279.4 %all-gather.11.cloned.1.call-start = ((), (), s32[]{:S(2)}) async-start(), calls=%async_computation.10 | async-start | bytes 5242880 | tf_op jit(solution)/shard_map/all_gather | solution.py:322
  580.9 341.7 %all-reduce.2.cloned.1.call-start = ((), (), s32[]{:S(2)}) async-start(), calls=%async_computation.12 | async-start | bytes 1048576 | tf_op jit(solution)/shard_map/psum | solution.py:331
  586.9 48.7 %collective-permute-start.43 = (bf16[1024,1024]{0,1:T(8,128)(2,1)}, bf16[1024,1024]{0,1:T(8,128)(2,1)S(1)}, u32[]{:S(2)}, u32[]{:S(2)}) collective-permute-start(bf16[1024,1024]{0,1:T(8,128)(2,1)} %convolution_convert_fusion.2), channel_id=1, source_target_pairs={{0,4},{4,0},{8,12},{12,8},{16,20},{20,16},{24,28},{28,24},{1,5},{5... | collective-permute-start | bytes 6291464 | tf_op jit(solution)/shard_map/ppermute | solution.py:166
  594.1 86.5 %collective-permute-start.39 = (bf16[1024,1024]{0,1:T(8,128)(2,1)S(1)}, bf16[1024,1024]{0,1:T(8,128)(2,1)S(1)}, u32[]{:S(2)}, u32[]{:S(2)}) collective-permute-start(bf16[1024,1024]{0,1:T(8,128)(2,1)S(1)} %convolution_convert_fusion.3), channel_id=1, source_target_pairs={{0,4},{4,0},{8,12},{12,8},{16,20},{20,16},{24,28},{28,24},{1,5},{5... | collective-permute-start | bytes 6291464 | tf_op jit(solution)/shard_map/ppermute | solution.py:166
  597.2 128.3 %collective-permute-start.51 = (bf16[1024,1024]{1,0:T(8,128)(2,1)S(1)}, bf16[1024,1024]{1,0:T(8,128)(2,1)S(1)}, u32[]{:S(2)}, u32[]{:S(2)}) collective-permute-start(bf16[1024,1024]{1,0:T(8,128)(2,1)S(1)} %convolution_convert_fusion), channel_id=1, source_target_pairs={{0,4},{4,0},{8,12},{12,8},{16,20},{20,16},{24,28},{28,24},{1,5},{5... | collective-permute-start | bytes 6291464 | tf_op jit(solution)/shard_map/ppermute | solution.py:166
  601.1 168.1 %collective-permute-start.47 = (bf16[1024,1024]{1,0:T(8,128)(2,1)S(1)}, bf16[1024,1024]{1,0:T(8,128)(2,1)S(1)}, u32[]{:S(2)}, u32[]{:S(2)}) collective-permute-start(bf16[1024,1024]{1,0:T(8,128)(2,1)S(1)} %convolution_convert_fusion.1), channel_id=1, source_target_pairs={{0,4},{4,0},{8,12},{12,8},{16,20},{20,16},{24,28},{28,24},{1,5},{5... | collective-permute-start | bytes 6291464 | tf_op jit(solution)/shard_map/ppermute | solution.py:166
  638.3 140.2 %collective-permute-start.46 = (bf16[256,1024]{0,1:T(8,128)(2,1)S(1)}, bf16[256,1024]{0,1:T(8,128)(2,1)S(1)}, u32[]{:S(2)}, u32[]{:S(2)}) collective-permute-start(bf16[256,1024]{0,1:T(8,128)(2,1)S(1)} %get-tuple-element.505), channel_id=1, source_target_pairs={{0,24},{4,28},{8,16},{12,20},{16,8},{20,12},{24,0},{28,4},{1,25},{... | collective-permute-start | bytes 1572872 | tf_op jit(solution)/shard_map/ppermute | solution.py:166
  639.9 139.1 %collective-permute-start.45 = (bf16[256,1024]{0,1:T(8,128)(2,1)S(1)}, bf16[256,1024]{0,1:T(8,128)(2,1)S(1)}, u32[]{:S(2)}, u32[]{:S(2)}) collective-permute-start(bf16[256,1024]{0,1:T(8,128)(2,1)S(1)} %get-tuple-element.506), channel_id=1, source_target_pairs={{0,16},{4,20},{8,24},{12,28},{16,0},{20,4},{24,8},{28,12},{1,17},{... | collective-permute-start | bytes 1572872 | tf_op jit(solution)/shard_map/ppermute | solution.py:166
  680.6 99.0 %collective-permute-start.44 = (bf16[256,1024]{0,1:T(8,128)(2,1)S(1)}, bf16[256,1024]{0,1:T(8,128)(2,1)S(1)}, u32[]{:S(2)}, u32[]{:S(2)}) collective-permute-start(bf16[256,1024]{0,1:T(8,128)(2,1)S(1)} %get-tuple-element.504), channel_id=1, source_target_pairs={{0,8},{4,12},{8,0},{12,4},{16,24},{20,28},{24,16},{28,20},{1,9},{5... | collective-permute-start | bytes 1572872 | tf_op jit(solution)/shard_map/ppermute | solution.py:166
  725.5 142.4 %collective-permute-start.42 = (bf16[256,1024]{0,1:T(8,128)(2,1)}, bf16[256,1024]{0,1:T(8,128)(2,1)}, u32[]{:S(2)}, u32[]{:S(2)}) collective-permute-start(bf16[256,1024]{0,1:T(8,128)(2,1)} %get-tuple-element.502), channel_id=1, source_target_pairs={{0,24},{4,28},{8,16},{12,20},{16,8},{20,12},{24,0},{28,4},{1,25},{... | collective-permute-start | bytes 1572872 | tf_op jit(solution)/shard_map/ppermute | solution.py:166
  769.1 98.8 %collective-permute-start.41 = (bf16[256,1024]{0,1:T(8,128)(2,1)}, bf16[256,1024]{0,1:T(8,128)(2,1)}, u32[]{:S(2)}, u32[]{:S(2)}) collective-permute-start(bf16[256,1024]{0,1:T(8,128)(2,1)} %get-tuple-element.503), channel_id=1, source_target_pairs={{0,16},{4,20},{8,24},{12,28},{16,0},{20,4},{24,8},{28,12},{1,17},{... | collective-permute-start | bytes 1572872 | tf_op jit(solution)/shard_map/ppermute | solution.py:166
  778.5 90.0 %collective-permute-start.40 = (bf16[256,1024]{0,1:T(8,128)(2,1)}, bf16[256,1024]{0,1:T(8,128)(2,1)}, u32[]{:S(2)}, u32[]{:S(2)}) collective-permute-start(bf16[256,1024]{0,1:T(8,128)(2,1)} %get-tuple-element.501), channel_id=1, source_target_pairs={{0,8},{4,12},{8,0},{12,4},{16,24},{20,28},{24,16},{28,20},{1,9},{5... | collective-permute-start | bytes 1572872 | tf_op jit(solution)/shard_map/ppermute | solution.py:166
  779.0 95.2 %collective-permute-start.54 = (bf16[1024,256]{1,0:T(8,128)(2,1)}, bf16[1024,256]{1,0:T(8,128)(2,1)}, u32[]{:S(2)}, u32[]{:S(2)}) collective-permute-start(bf16[1024,256]{1,0:T(8,128)(2,1)} %get-tuple-element.499), channel_id=1, source_target_pairs={{0,24},{4,28},{8,16},{12,20},{16,8},{20,12},{24,0},{28,4},{1,25},{... | collective-permute-start | bytes 1572872 | tf_op jit(solution)/shard_map/ppermute | solution.py:166
  779.6 96.7 %collective-permute-start.53 = (bf16[1024,256]{1,0:T(8,128)(2,1)}, bf16[1024,256]{1,0:T(8,128)(2,1)}, u32[]{:S(2)}, u32[]{:S(2)}) collective-permute-start(bf16[1024,256]{1,0:T(8,128)(2,1)} %get-tuple-element.500), channel_id=1, source_target_pairs={{0,16},{4,20},{8,24},{12,28},{16,0},{20,4},{24,8},{28,12},{1,17},{... | collective-permute-start | bytes 1572872 | tf_op jit(solution)/shard_map/ppermute | solution.py:166
  858.6 154.4 %reduce-scatter.11.cloned.1.call-start = ((), (), s32[]{:S(2)}) async-start(), calls=%async_computation.11 | async-start | bytes 5242880 | tf_op jit(solution)/shard_map/reduce_scatter | solution.py:344
  867.9 25.0 %collective-permute-start.52 = (bf16[1024,256]{1,0:T(8,128)(2,1)}, bf16[1024,256]{1,0:T(8,128)(2,1)}, u32[]{:S(2)}, u32[]{:S(2)}) collective-permute-start(bf16[1024,256]{1,0:T(8,128)(2,1)} %get-tuple-element.498), channel_id=1, source_target_pairs={{0,8},{4,12},{8,0},{12,4},{16,24},{20,28},{24,16},{28,20},{1,9},{5... | collective-permute-start | bytes 1572872 | tf_op jit(solution)/shard_map/ppermute | solution.py:166
  868.0 37.6 %collective-permute-start.50 = (bf16[1024,256]{1,0:T(8,128)(2,1)}, bf16[1024,256]{1,0:T(8,128)(2,1)}, u32[]{:S(2)}, u32[]{:S(2)}) collective-permute-start(bf16[1024,256]{1,0:T(8,128)(2,1)} %get-tuple-element.496), channel_id=1, source_target_pairs={{0,24},{4,28},{8,16},{12,20},{16,8},{20,12},{24,0},{28,4},{1,25},{... | collective-permute-start | bytes 1572872 | tf_op jit(solution)/shard_map/ppermute | solution.py:166
  868.5 43.0 %collective-permute-start.49 = (bf16[1024,256]{1,0:T(8,128)(2,1)}, bf16[1024,256]{1,0:T(8,128)(2,1)}, u32[]{:S(2)}, u32[]{:S(2)}) collective-permute-start(bf16[1024,256]{1,0:T(8,128)(2,1)} %get-tuple-element.497), channel_id=1, source_target_pairs={{0,16},{4,20},{8,24},{12,28},{16,0},{20,4},{24,8},{28,12},{1,17},{... | collective-permute-start | bytes 1572872 | tf_op jit(solution)/shard_map/ppermute | solution.py:166
  874.3 39.3 %collective-permute-start.48 = (bf16[1024,256]{1,0:T(8,128)(2,1)}, bf16[1024,256]{1,0:T(8,128)(2,1)}, u32[]{:S(2)}, u32[]{:S(2)}) collective-permute-start(bf16[1024,256]{1,0:T(8,128)(2,1)} %get-tuple-element.495), channel_id=1, source_target_pairs={{0,8},{4,12},{8,0},{12,4},{16,24},{20,28},{24,16},{28,20},{1,9},{5... | collective-permute-start | bytes 1572872 | tf_op jit(solution)/shard_map/ppermute | solution.py:166
  921.1 26.3 %collective-permute-start.35 = (bf16[512,1024]{1,0:T(8,128)(2,1)}, bf16[512,1024]{1,0:T(8,128)(2,1)}, u32[]{:S(2)}, u32[]{:S(2)}) collective-permute-start(bf16[512,1024]{1,0:T(8,128)(2,1)} %fusion.121), channel_id=1, source_target_pairs={{0,4},{4,0},{8,12},{12,8},{16,20},{20,16},{24,28},{28,24},{1,5},{5... | collective-permute-start | bytes 3145736 | tf_op jit(solution)/shard_map/ppermute | solution.py:166
  927.3 50.1 %collective-permute-start.31 = (bf16[1024,768]{1,0:T(8,128)(2,1)}, bf16[1024,768]{1,0:T(8,128)(2,1)}, u32[]{:S(2)}, u32[]{:S(2)}) collective-permute-start(bf16[1024,768]{1,0:T(8,128)(2,1)} %fusion.114), channel_id=1, source_target_pairs={{0,4},{4,0},{8,12},{12,8},{16,20},{20,16},{24,28},{28,24},{1,5},{5... | collective-permute-start | bytes 4718600 | tf_op jit(solution)/shard_map/ppermute | solution.py:166
  950.7 33.9 %collective-permute-start.38 = (bf16[512,256]{1,0:T(8,128)(2,1)S(1)}, bf16[512,256]{1,0:T(8,128)(2,1)S(1)}, u32[]{:S(2)}, u32[]{:S(2)}) collective-permute-start(bf16[512,256]{1,0:T(8,128)(2,1)S(1)} %get-tuple-element.513), channel_id=1, source_target_pairs={{0,24},{4,28},{8,16},{12,20},{16,8},{20,12},{24,0},{28,4},{1,25},{... | collective-permute-start | bytes 786440 | tf_op jit(solution)/shard_map/ppermute | solution.py:166
  950.8 35.3 %collective-permute-start.37 = (bf16[512,256]{1,0:T(8,128)(2,1)S(1)}, bf16[512,256]{1,0:T(8,128)(2,1)S(1)}, u32[]{:S(2)}, u32[]{:S(2)}) collective-permute-start(bf16[512,256]{1,0:T(8,128)(2,1)S(1)} %get-tuple-element.514), channel_id=1, source_target_pairs={{0,16},{4,20},{8,24},{12,28},{16,0},{20,4},{24,8},{28,12},{1,17},{... | collective-permute-start | bytes 786440 | tf_op jit(solution)/shard_map/ppermute | solution.py:166
  954.7 31.5 %collective-permute-start.36 = (bf16[512,256]{1,0:T(8,128)(2,1)S(1)}, bf16[512,256]{1,0:T(8,128)(2,1)S(1)}, u32[]{:S(2)}, u32[]{:S(2)}) collective-permute-start(bf16[512,256]{1,0:T(8,128)(2,1)S(1)} %get-tuple-element.512), channel_id=1, source_target_pairs={{0,8},{4,12},{8,0},{12,4},{16,24},{20,28},{24,16},{28,20},{1,9},{5... | collective-permute-start | bytes 786440 | tf_op jit(solution)/shard_map/ppermute | solution.py:166
  980.7 26.2 %collective-permute-start.34 = (bf16[256,768]{1,0:T(8,128)(2,1)S(1)}, bf16[256,768]{1,0:T(8,128)(2,1)S(1)}, u32[]{:S(2)}, u32[]{:S(2)}) collective-permute-start(bf16[256,768]{1,0:T(8,128)(2,1)S(1)} %get-tuple-element.508), channel_id=1, source_target_pairs={{0,24},{4,28},{8,16},{12,20},{16,8},{20,12},{24,0},{28,4},{1,25},{... | collective-permute-start | bytes 1179656 | tf_op jit(solution)/shard_map/ppermute | solution.py:166
  980.8 30.4 %collective-permute-start.33 = (bf16[256,768]{1,0:T(8,128)(2,1)S(1)}, bf16[256,768]{1,0:T(8,128)(2,1)S(1)}, u32[]{:S(2)}, u32[]{:S(2)}) collective-permute-start(bf16[256,768]{1,0:T(8,128)(2,1)S(1)} %get-tuple-element.509), channel_id=1, source_target_pairs={{0,16},{4,20},{8,24},{12,28},{16,0},{20,4},{24,8},{28,12},{1,17},{... | collective-permute-start | bytes 1179656 | tf_op jit(solution)/shard_map/ppermute | solution.py:166
  984.7 26.6 %collective-permute-start.32 = (bf16[256,768]{1,0:T(8,128)(2,1)S(1)}, bf16[256,768]{1,0:T(8,128)(2,1)S(1)}, u32[]{:S(2)}, u32[]{:S(2)}) collective-permute-start(bf16[256,768]{1,0:T(8,128)(2,1)S(1)} %get-tuple-element.507), channel_id=1, source_target_pairs={{0,8},{4,12},{8,0},{12,4},{16,24},{20,28},{24,16},{28,20},{1,9},{5... | collective-permute-start | bytes 1179656 | tf_op jit(solution)/shard_map/ppermute | solution.py:166
  1021.9 4.4 collective-permute-start.26
  1022.0 5.6 collective-permute-start.25
  1022.4 5.3 collective-permute-start.24
  1027.7 4.8 collective-permute-start.27
  1032.6 7.5 collective-permute-start.30
  1034.4 9.3 collective-permute-start.29
  1038.7 5.0 collective-permute-start.28
  (151 other events, 3528.3 us)
Sparse Core Ops, SparseCore 0:
  13.3 36.1 all-gather.4
  145.5 46.4 reduce-scatter.4
  193.5 34.9 all-gather.8
  230.5 34.9 all-gather.6
  486.6 43.1 reduce-scatter.8
  532.1 44.3 reduce-scatter.6
  581.0 34.9 all-gather.10
  858.7 31.5 all-reduce.1
  892.9 44.3 reduce-scatter.10
